TPU v7x, 128 devices: a whole 4x4x4 slice. The times are simulated.
128 devices in a mesh: row: 8 (over x, core), col: 16 (over z, y).
Axes of the slice: x: 4, y: 4, z: 4, core: 2. Of those that a mesh axis runs over, the one named last changes fastest.
Arguments:
- density_tiles: float32 [3, 4096, 4096], P(None, ('row', 'col')), may hold values from -0.012 to 0.012
- tile_ids: int32 [4096], P(('row', 'col')), may hold values from 0 to 16383, as said below
- batch_blocks: int32 [128, 8], replicated, may hold values from 0 to 127, as said below
- basis_values: float32 [128, 512, 1024], P(('row', 'col')), may hold values from -6 to 6
- grid_weight: float32 [128, 1024], P(('row', 'col')), may hold values from 0.0002 to 0.002
- xc_kernel: float32 [128, 1024], P(('row', 'col')), may hold values from -2 to -0.5
- grid_coord: float32 [3, 128, 1024], P(None, ('row', 'col')), may hold values from -1 to 1
- orbitals: float32 [8192, 512], P('row'), may hold values from -1.5 to 1.5
- precond_diag: float32 [8192], P('row'), may hold values from 1 to 4
- orbital_energy: float32 [512], replicated, may hold values from -3 to -0.5
Outputs:
- new_density: float32 [3, 4096, 4096], P(None, ('row', 'col'))
Inputs may be any that keep to these rules, and one draw needn't show every extreme that they name: `tile_ids`: the 32 slots of device (r, c), counted in row+col order, list distinct tiles I * 128 + J with I in the r-th range of 16 blocks and J in the c-th range of 8 blocks. `batch_blocks`: each row holds 8 ascending blocks, no two in the same range of 8 blocks, and exactly 1 of them in each range of 16 blocks.
All inputs are finite; a program needn't handle non-finite values.
Results may differ from a plain program's by a relative error of at most 0.0003.
Values sent between devices are 32-bit elements; how exact they have to be, the bound alone decides.
A program may use at most 128 MiB of HBM per device.

v0:
```python
import jax
import jax.numpy as jnp
from jax import lax
from jax.sharding import PartitionSpec as P

NB = 8192
TILE = 64
FB = 8


PRECISE = lax.Precision.HIGHEST


def from_root(value, axis, source):
    kept = jnp.where(lax.axis_index(axis) == source, value, 0).astype(value.dtype)
    return lax.psum(kept, axis)


def slot_plan(blocks, owner_row, owner_col, col_blocks, per_range):
    matched = blocks // col_blocks == owner_col[..., None]
    active = jnp.any(matched, axis=-1)
    positions = jnp.arange(blocks.shape[-1], dtype=jnp.int32)
    column_place = jnp.sum(jnp.where(matched, positions, 0), axis=-1)
    row_place = owner_row[..., None] * per_range + jnp.arange(per_range, dtype=jnp.int32)
    return (active, row_place, column_place)


def local(
    density_tiles,
    tile_ids,
    batch_blocks,
    basis_values,
    grid_weight,
    xc_kernel,
    grid_coord,
    orbitals,
    precond_diag,
    orbital_energy,
):
    row_count = lax.axis_size("row")
    col_count = lax.axis_size("col")
    device_count = row_count * col_count
    own_row = lax.axis_index("row")
    own_col = lax.axis_index("col")
    own_index = own_row * col_count + own_col
    block_count = NB // TILE
    row_blocks = block_count // row_count
    col_blocks = block_count // col_count
    per_range = FB // row_count
    batch_count = basis_values.shape[0]
    slot_count = batch_count * per_range
    tile_area = TILE * TILE
    tile_local = tile_ids.shape[0]
    orbital_count = orbitals.shape[1]
    col_ratio = col_count // row_count
    col_width = col_blocks * TILE
    batch_width = FB * TILE
    orbital_piece = lax.dynamic_slice_in_dim(
        orbitals, own_col % col_ratio * col_width, col_width, 0
    )
    orbital_cols = from_root(orbital_piece, "row", own_col // col_ratio)
    requests = batch_blocks.reshape(device_count, batch_count, FB)
    owner_rows = jnp.full((device_count, batch_count), own_row, dtype=jnp.int32)
    owner_cols = jnp.full((device_count, batch_count), own_col, dtype=jnp.int32)
    active, row_place, column_place = slot_plan(
        requests, owner_rows, owner_cols, col_blocks, per_range
    )
    want_rows = jnp.take_along_axis(requests, row_place, axis=2)
    want_col = jnp.take_along_axis(requests, column_place[..., None], axis=2)
    wanted = jnp.where(active[..., None], want_rows * block_count + want_col, -1).reshape(-1)
    selector = (wanted[:, None] == tile_ids[None, :]).astype(jnp.float32)
    outgoing = jnp.einsum("ns,dsx->dnx", selector, density_tiles, precision=PRECISE)
    arrived = lax.all_to_all(outgoing, ("row", "col"), split_axis=1, concat_axis=1, tiled=True)
    own_blocks = lax.dynamic_slice_in_dim(requests, own_index, 1, 0)[0]
    block_pos = jnp.arange(FB, dtype=jnp.int32)
    batch_pos = jnp.arange(batch_count, dtype=jnp.int32)
    source = (block_pos // per_range)[None, :, None] * col_count + (own_blocks // col_blocks)[
        :, None, :
    ]
    lookup = (
        source * slot_count
        + batch_pos[:, None, None] * per_range
        + (block_pos % per_range)[None, :, None]
    )
    density = jnp.take(arrived, lookup.reshape(-1), axis=1).reshape(
        3, batch_count, FB, FB, TILE, TILE
    )
    density = density.transpose(0, 1, 2, 4, 3, 5).reshape(3, batch_count, batch_width, batch_width)
    projected = jnp.einsum("dkmn,knp->dkmp", density, basis_values, precision=PRECISE)
    response = jnp.sum(basis_values[None] * projected, axis=2)
    potential = xc_kernel[None] * response + grid_coord
    weighted = basis_values[None] * (grid_weight[None] * potential)[:, :, None, :]
    hamiltonian = jnp.einsum("dkmp,knp->dkmn", weighted, basis_values, precision=PRECISE)
    ham_tiles = (
        hamiltonian.reshape(3, batch_count, FB, TILE, FB, TILE)
        .transpose(0, 1, 2, 4, 3, 5)
        .reshape(3, batch_count * FB * FB, tile_area)
    )
    owners = jnp.arange(device_count, dtype=jnp.int32)
    target_rows = (owners // col_count)[:, None]
    target_cols = (owners % col_count)[:, None]
    mine_all = jnp.broadcast_to(own_blocks[None], (device_count, batch_count, FB))
    back_active, back_rows, back_col = slot_plan(
        mine_all, target_rows, target_cols, col_blocks, per_range
    )
    pick_index = (batch_pos[None, :, None] * FB + back_rows) * FB + back_col[..., None]
    keep_mask = back_active[..., None].reshape(-1)
    returning = jnp.where(
        keep_mask[None, :, None], jnp.take(ham_tiles, pick_index.reshape(-1), axis=1), 0.0
    )
    returned = lax.all_to_all(returning, ("row", "col"), split_axis=1, concat_axis=1, tiled=True)
    ham_listed = jnp.einsum("ns,dnx->dsx", selector, returned, precision=PRECISE)
    local_rows = tile_ids // block_count - own_row * row_blocks
    local_cols = tile_ids % block_count - own_col * col_blocks
    row_hot = (local_rows[None, :] == jnp.arange(row_blocks, dtype=jnp.int32)[:, None]).astype(
        jnp.float32
    )
    col_hot = (local_cols[None, :] == jnp.arange(col_blocks, dtype=jnp.int32)[:, None]).astype(
        jnp.float32
    )
    block_matrix = jnp.einsum(
        "rs,cs,dsab->dracb",
        row_hot,
        col_hot,
        ham_listed.reshape(3, tile_local, TILE, TILE),
        precision=PRECISE,
    )
    block_matrix = block_matrix.reshape(3, row_blocks * TILE, col_width)
    partial_rows = jnp.einsum("drc,co->dro", block_matrix, orbital_cols, precision=PRECISE)
    summed_rows = lax.psum(partial_rows, "col")
    response_orbs = -summed_rows / (precond_diag[:, None] - orbital_energy[None, :])
    response_piece = lax.dynamic_slice_in_dim(
        response_orbs, own_col % col_ratio * col_width, col_width, 1
    )
    response_cols = from_root(response_piece, "row", own_col // col_ratio)
    x_rows = jnp.take(response_orbs.reshape(3, row_blocks, TILE, orbital_count), local_rows, axis=1)
    c_rows = jnp.take(orbitals.reshape(row_blocks, TILE, orbital_count), local_rows, axis=0)
    x_cols = jnp.take(response_cols.reshape(3, col_blocks, TILE, orbital_count), local_cols, axis=1)
    c_cols = jnp.take(orbital_cols.reshape(col_blocks, TILE, orbital_count), local_cols, axis=0)
    renewed = jnp.einsum("dsao,sbo->dsab", x_rows, c_cols, precision=PRECISE)
    renewed = renewed + jnp.einsum("sao,dsbo->dsab", c_rows, x_cols, precision=PRECISE)
    return renewed.reshape(3, tile_local, tile_area)


def solution(mesh):
    placed = (
        P(None, ("row", "col"), None),
        P(("row", "col")),
        P(),
        P(("row", "col"), None, None),
        P(("row", "col"), None),
        P(("row", "col"), None),
        P(None, ("row", "col"), None),
        P("row", None),
        P("row"),
        P(),
    )
    return jax.shard_map(
        local, mesh=mesh, in_specs=placed, out_specs=P(None, ("row", "col"), None), check_vma=False
    )
```

profile of v0, /device:TPU:1, one launch (start us, length us, event | category | flops | bytes accessed | tf_op | source)
XLA Modules:
  0.0 685.2 jit_solution(637120942322534087)
XLA Ops:
  15.5 7.5 %copy.47 = f32[3,128,4096]{2,0,1:T(4,128)} copy(f32[3,128,4096]{2,1,0:T(8,128)S(1)} %convolution_bitcast_fusion) | data formatting | bytes 12582912 | tf_op jit(solution)/shard_map/ns,dsx->dnx/transpose | solution.py:72
  23.1 12.6 %all-to-all-start = ((f32[3,128,4096]{2,0,1:T(4,128)}), f32[3,128,4096]{2,0,1:T(4,128)}, u32[]{:S(2)}, u32[]{:S(2)}) async-start(f32[3,128,4096]{2,0,1:T(4,128)} %copy.47), calls=%async_computation | async-start | bytes 16777216 | tf_op jit(solution)/shard_map/all_to_all | solution.py:73
  36.1 100.6 %all-to-all-done = f32[3,128,4096]{2,0,1:T(4,128)} async-done(((f32[3,128,4096]{2,0,1:T(4,128)}), f32[3,128,4096]{2,0,1:T(4,128)}, u32[]{:S(2)}, u32[]{:S(2)}) %all-to-all-start) | async-done | bytes 6291488 | tf_op jit(solution)/shard_map/all_to_all | solution.py:73
  136.8 8.1 %gather_fusion.1 = f32[64,3,4096]{2,1,0:T(4,128)} fusion(f32[3,128,4096]{2,0,1:T(4,128)} %all-to-all-done, s32[1024]{0:T(1024)S(1)} %pad_clamp_fusion.2), kind=kCustom, calls=%fused_computation.3 | custom fusion | bytes 6291712 | tf_op jit(solution)/shard_map/jit(_take)/gather | solution.py:85
  160.3 8.1 %copy.49 = f32[3,1,8,64,8,64]{5,4,3,2,0,1:T(8,128)} copy(f32[3,1,8,64,8,64]{5,3,4,2,0,1:T(8,128)S(1)} %select_bitcast_fusion.1) | data formatting | bytes 6291456 | tf_op jit(solution)/shard_map/transpose | solution.py:88
  168.4 6.4 reshape.542
  174.9 13.6 %fusion.6 = f32[3,1024]{1,0:T(4,128)S(1)} fusion(f32[512,1024]{1,0:T(8,128)} %bitcast.155, f32[3,512,512]{2,1,0:T(8,128)} %reshape.542, f32[1,512,1024]{2,1,0:T(8,128)} %param.15), kind=kOutput, calls=%fused_computation.16 | convolution fusion | flops 9666819072 | bytes 7352320 | tf_op jit(solution)/shard_map/dkmn,knp->dkmp/dot_general | solution.py:89
  188.5 11.9 %fusion.32 = f32[3,1,512,512]{3,2,0,1:T(8,128)} fusion(f32[1,512,1024]{2,1,0:T(8,128)S(1)} %copy-done.12, f32[3,1024]{1,0:T(4,128)S(1)} %bitcast.152, f32[512,1024]{1,0:T(8,128)S(1)} %bitcast.156), kind=kOutput, calls=%fused_computation.47 | convolution fusion | flops 9665249280 | bytes 7352320 | tf_op jit(solution)/shard_map/dkmp,knp->dkmn/dot_general | solution.py:93
  206.2 6.6 copy.70
  224.7 11.9 %gather_fusion.2 = f32[128,3,4096]{2,1,0:T(4,128)} fusion(f32[3,64,4096]{2,0,1:T(4,128)} %copy.51, s32[1024]{0:T(1024)S(1)} %pad_clamp_fusion.1), kind=kCustom, calls=%fused_computation.4 | custom fusion | bytes 12583424 | tf_op jit(solution)/shard_map/jit(_take)/gather | solution.py:109
  236.6 11.6 %select_bitcast_fusion = f32[3,128,4096]{2,0,1:T(4,128)} fusion(f32[128,3,4096]{2,1,0:T(4,128)} %gather_fusion.2, pred[128]{0:T(512)(128)(4,1)S(1)} %fusion.61, pred[128]{0:T(512)(128)(4,1)S(1)} %compare_and_fusion), kind=kLoop, calls=%fused_computation.14 | loop fusion | flops 3145728 | bytes 12583168 | tf_op jit(solution)/shard_map/jit(_where)/select_n | solution.py:108
  248.3 10.8 %all-to-all-start.1 = ((f32[3,128,4096]{2,0,1:T(4,128)}), f32[3,128,4096]{2,0,1:T(4,128)}, u32[]{:S(2)}, u32[]{:S(2)}) async-start(f32[3,128,4096]{2,0,1:T(4,128)} %select_bitcast_fusion), calls=%async_computation.1 | async-start | bytes 16777216 | tf_op jit(solution)/shard_map/all_to_all | solution.py:111
  261.6 104.2 %all-to-all-done.1 = f32[3,128,4096]{2,0,1:T(4,128)} async-done(((f32[3,128,4096]{2,0,1:T(4,128)}), f32[3,128,4096]{2,0,1:T(4,128)}, u32[]{:S(2)}, u32[]{:S(2)}) %all-to-all-start.1) | async-done | bytes 6291488 | tf_op jit(solution)/shard_map/all_to_all | solution.py:111
  365.8 8.8 %fusion.15 = f32[3,32,4096]{2,1,0:T(8,128)S(1)} fusion(f32[3,128,4096]{2,0,1:T(4,128)} %all-to-all-done.1, s32[128]{0:T(128)S(1)} %fusion.77, s32[32]{0:T(128)S(1)} %copy-done.7), kind=kOutput, calls=%fused_computation.29 | convolution fusion | flops 603983872 | bytes 7864960 | tf_op jit(solution)/shard_map/ns,dnx->dsx/dot_general | solution.py:112
  377.1 15.5 %convolution_bitcast_fusion.1 = f32[3,16,64,8,64]{4,1,2,0,3:T(8,128)} fusion(f32[3,32,64,64]{3,2,1,0:T(8,128)} %reshape.545, f32[32,16]{0,1:T(8,128)S(1)} %convert_bitcast_fusion, f32[32,8]{0,1:T(8,128)S(1)} %convert_bitcast_fusion.1), kind=kOutput, calls=%fused_computation.30 | convolution fusion | flops 603983872 | bytes 7867392 | tf_op jit(solution)/shard_map/rs,cs,dsab->dracb/dot_general | solution.py:121
  392.6 16.3 %copy.54 = f32[3,16,64,8,64]{4,3,2,1,0:T(8,128)} copy(f32[3,16,64,8,64]{4,1,2,0,3:T(8,128)} %convolution_bitcast_fusion.1) | data formatting | bytes 12582912 | tf_op jit(solution)/shard_map/rs,cs,dsab->dracb/transpose | solution.py:121
  408.9 11.5 %reshape.546 = f32[3,1024,512]{2,1,0:T(8,128)} reshape(f32[3,16,64,8,64]{4,3,2,1,0:T(8,128)} %copy.54) | data formatting | bytes 12582912 | tf_op jit(solution)/shard_map/reshape | solution.py:128
  420.4 13.5 %fusion.41 = f32[3,1024,512]{2,1,0:T(8,128)} fusion(f32[3,1024,512]{2,1,0:T(8,128)} %reshape.546, f32[512,512]{1,0:T(8,128)} %all-reduce.4.cloned.1.call-done), kind=kOutput, calls=%fused_computation.48 | convolution fusion | flops 9663676416 | bytes 13631488 | tf_op jit(solution)/shard_map/drc,co->dro/dot_general | solution.py:129
  436.2 120.8 %all-reduce.6.cloned.1.call-done = f32[3,1024,512]{2,1,0:T(8,128)} async-done(((f32[3,1024,512]{2,1,0:T(8,128)}), f32[3,1024,512]{2,1,0:T(8,128)}) %all-reduce.6.cloned.1.call-update) | async-done | bytes 6291472 | tf_op jit(solution)/shard_map/psum | solution.py:130
  573.3 9.0 %gather_fusion.3 = f32[32,3,64,512]{3,2,1,0:T(8,128)} fusion(f32[3,16,64,512]{3,2,1,0:T(8,128)} %bitcast.146, s32[1024]{0:T(1024)S(1)} %pad_clamp_fusion), kind=kCustom, calls=%fused_computation.5 | custom fusion | bytes 25165952 | tf_op jit(solution)/shard_map/jit(_take)/gather | solution.py:136
  582.3 50.9 %all-reduce.8.cloned.1.call-done = f32[3,8,64,512]{3,2,1,0:T(8,128)} async-done(((f32[3,8,64,512]{3,2,1,0:T(8,128)}), f32[3,8,64,512]{3,2,1,0:T(8,128)}) %all-reduce.8.cloned.1.call-update) | async-done | bytes 3145744 | tf_op jit(solution)/shard_map/psum | solution.py:16
  633.2 7.7 %gather_fusion.4 = f32[32,3,64,512]{3,2,1,0:T(8,128)} fusion(f32[3,8,64,512]{3,2,1,0:T(8,128)} %all-reduce.8.cloned.1.call-done, s32[1024]{0:T(1024)S(1)} %pad_clamp_fusion.3), kind=kCustom, calls=%fused_computation.6 | custom fusion | bytes 25165952 | tf_op jit(solution)/shard_map/jit(_take)/gather | solution.py:138
  640.9 15.3 %fusion = f32[32,3,64,64]{3,2,1,0:T(8,128)S(1)} fusion(f32[32,3,64,512]{3,2,1,0:T(8,128)} %gather_fusion.4, pred[32]{0:T(512)(128)(4,1)S(1)} %get-tuple-element.10, f32[32,64,512]{2,1,0:T(8,128)} %gather_fusion.5, pred[32]{0:T(512)(128)(4,1)S(1)} %get-tuple-element.16), kind=kOutput, calls=%fused_computation.8 | convolution fusion | flops 2420113408 | bytes 18350144 | tf_op jit(solution)/shard_map/sao,dsbo->dsab/dot_general | solution.py:141
  656.3 15.4 %bitcast_add_fusion = f32[3,32,64,64]{2,3,0,1:T(8,128)} fusion(f32[32,3,64,64]{3,2,1,0:T(8,128)S(1)} %fusion, f32[32,3,64,512]{3,2,1,0:T(8,128)S(1)} %copy-done.3, pred[32]{0:T(512)(128)(4,1)S(1)} %get-tuple-element.16, f32[32,64,512]{2,1,0:T(8,128)S(1)} %copy-done.5, pred[32]{0:T(512)(128)(4,1)S(1)} %get-tuple-element.10), kind=kOutput, calls=%fused_computation.35 | convolution fusion | flops 2420506624 | bytes 19923008 | tf_op jit(solution)/shard_map/dsao,sbo->dsab/dot_general | solution.py:140
  (85 shorter events, 72.8 us)
Async XLA Ops:
  6.5 5.6 copy-start
  23.1 113.7 %all-to-all-start = ((f32[3,128,4096]{2,0,1:T(4,128)}), f32[3,128,4096]{2,0,1:T(4,128)}, u32[]{:S(2)}, u32[]{:S(2)}) async-start(f32[3,128,4096]{2,0,1:T(4,128)} %copy.47), calls=%async_computation | async-start | bytes 16777216 | tf_op jit(solution)/shard_map/all_to_all | solution.py:73
  174.9 13.6 %copy-start.6 = (f32[3,1,1024]{2,1,0:T(1,128)S(1)}, f32[3,1,1024]{2,1,0:T(1,128)}, u32[]{:S(2)}) copy-start(f32[3,1,1024]{2,1,0:T(1,128)} %param.18) | copy-start | bytes 36868
  174.9 13.6 %copy-start.9 = (f32[1,1024]{1,0:T(1,128)S(1)}, f32[1,1024]{1,0:T(1,128)}, u32[]{:S(2)}) copy-start(f32[1,1024]{1,0:T(1,128)} %param.17) | copy-start | bytes 12292
  174.9 13.6 %copy-start.10 = (f32[1,1024]{1,0:T(1,128)S(1)}, f32[1,1024]{1,0:T(1,128)}, u32[]{:S(2)}) copy-start(f32[1,1024]{1,0:T(1,128)} %param.16) | copy-start | bytes 12292
  174.9 13.7 %copy-start.12 = (f32[1,512,1024]{2,1,0:T(8,128)S(1)}, f32[1,512,1024]{2,1,0:T(8,128)}, u32[]{:S(2)}) copy-start(f32[1,512,1024]{2,1,0:T(8,128)} %param.15) | copy-start | bytes 6291460
  248.3 13.2 %copy-start.7 = (s32[32]{0:T(128)S(1)}, s32[32]{0:T(128)}, u32[]{:S(2)}) copy-start(s32[32]{0:T(128)} %param.13) | copy-start | bytes 388
  248.3 117.5 %all-to-all-start.1 = ((f32[3,128,4096]{2,0,1:T(4,128)}), f32[3,128,4096]{2,0,1:T(4,128)}, u32[]{:S(2)}, u32[]{:S(2)}) async-start(f32[3,128,4096]{2,0,1:T(4,128)} %select_bitcast_fusion), calls=%async_computation.1 | async-start | bytes 16777216 | tf_op jit(solution)/shard_map/all_to_all | solution.py:111
  259.1 161.3 %all-reduce.4.cloned.1.call-start = ((), (), s32[]{:S(2)}) async-start(), calls=%async_computation.2 | async-start | bytes 2097152 | tf_op jit(solution)/shard_map/psum | solution.py:16
  261.5 295.5 %all-reduce.6.cloned.1.call-start = ((), (), s32[]{:S(2)}) async-start(), calls=%async_computation.3 | async-start | bytes 12582912 | tf_op jit(solution)/shard_map/psum | solution.py:130
  433.9 0.7 copy-start.8
  433.9 0.7 copy-start.11
  433.9 199.3 %all-reduce.8.cloned.1.call-start = ((), (), s32[]{:S(2)}) async-start(), calls=%async_computation.4 | async-start | bytes 6291456 | tf_op jit(solution)/shard_map/psum | solution.py:16
  561.4 2.6 copy-start.2
  566.1 4.5 copy-start.4
  640.9 15.3 %copy-start.3 = (f32[32,3,64,512]{3,2,1,0:T(8,128)S(1)}, f32[32,3,64,512]{3,2,1,0:T(8,128)}, u32[]{:S(2)}) copy-start(f32[32,3,64,512]{3,2,1,0:T(8,128)} %gather_fusion.3) | copy-start | bytes 37748740
  640.9 15.3 %copy-start.5 = (f32[32,64,512]{2,1,0:T(8,128)S(1)}, f32[32,64,512]{2,1,0:T(8,128)}, u32[]{:S(2)}) copy-start(f32[32,64,512]{2,1,0:T(8,128)} %gather_fusion) | copy-start | bytes 12582916
  656.3 22.2 %copy-start.1 = (f32[3,32,4096]{2,1,0:T(8,128)S(1)}, f32[3,32,4096]{2,1,0:T(8,128)}, u32[]{:S(2)}) copy-start(f32[3,32,4096]{2,1,0:T(8,128)} %param.12) | copy-start | bytes 4718596
Sparse Core Ops, SparseCore 0:
  262.2 84.7 all-reduce.3
  434.1 122.8 all-reduce.5
  566.2 66.9 all-reduce.7
where the time goes:
time: 694 us; the launch traced here: 685 us
  waiting for transfers between devices  377 us (54%)
  local copies, waits for them, and re-layouts  146 us (21%)
  matrix products  97.3 us (14%)
  other arithmetic  27.9 us (4%)
  starting transfers between devices  23.9 us (3%)
  between operations  13.6 us (2%)
    psum x1, waiting for transfers between devices, local(): summed_rows = lax.psum(partial_rows, 'col')  121 us
    all_to_all x1, waiting for transfers between devices, local(): lax.all_to_all(returning, ('row', 'col'), split_axis=1, concat_axis=1, ti...  104 us
    all_to_all x1, waiting for transfers between devices, local(): lax.all_to_all(outgoing, ('row', 'col'), split_axis=1, concat_axis=1, til...  101 us
    psum x2, waiting for transfers between devices, from_root(): return lax.psum(kept, axis)  50.9 us
    gather x3, local copies, waits for them, and re-layouts, local(): jnp.take(arrived, lookup.reshape(-1), axis=1)  19.9 us
    transpose x1, local copies, waits for them, and re-layouts, local(): jnp.einsum('rs,cs,dsab->dracb', row_hot, col_hot, ham_listed.reshape(3, t...  16.3 us
    dot_general x1, matrix products, local(): jnp.einsum('rs,cs,dsab->dracb', row_hot, col_hot, ham_listed.reshape(3, t...  15.5 us
    dot_general x1, matrix products, local(): renewed = jnp.einsum('dsao,sbo->dsab', x_rows, c_cols, precision=PRECISE)  15.4 us
  transfers between devices with their start and end apart: 5, of which 4 were waited for; matrix products, arithmetic and copies ran while one was open for 11% of the time, Pallas kernels for 0%

commit v1 on v0

v1 whole, which is shorter than its diff:
```python
import jax
import jax.numpy as jnp
from jax import lax
from jax.experimental import pallas as pl
from jax.experimental.pallas import tpu as pltpu
from jax.sharding import PartitionSpec as P

TILE = 64
NBLK = 128
F32 = jnp.float32
BF16 = jnp.bfloat16
NT = (((1,), (1,)), ((), ()))


def split(x):
    hi = x.astype(BF16)
    lo = (x - hi.astype(F32)).astype(BF16)
    return hi, lo


def dot(a, b):
    return jnp.dot(a, b, preferred_element_type=F32)


def dot_nt(a, b):
    return lax.dot_general(a, b, NT, preferred_element_type=F32)


def vmem():
    return pl.BlockSpec(memory_space=pltpu.VMEM)


def smem():
    return pl.BlockSpec(memory_space=pltpu.SMEM)


def select_kernel(slot_ref, tiles_ref, out_ref):
    count = out_ref.shape[0]

    def body(n, carry):
        slot = slot_ref[n]
        found = jnp.where(slot >= 0, 1.0, 0.0).astype(F32)
        picked = tiles_ref[:, jnp.maximum(slot, 0)]
        out_ref[n] = picked * found
        return carry

    lax.fori_loop(0, count, body, 0)


def select_tiles(slots, tiles):
    return pl.pallas_call(
        select_kernel,
        out_shape=jax.ShapeDtypeStruct((slots.shape[0], 3, 32, 128), F32),
        in_specs=[smem(), vmem()],
        out_specs=vmem(),
        name="select_tiles",
    )(slots, tiles)


def batch_kernel(
    col_ref, mask_ref, t_ref, b_ref, gw_ref, xc_ref, gc_ref, c_ref, out_ref,
    bperm, plane, bstack, bside, dcat, acat, hcat, ccat, pot,
):
    for i in range(8):
        rows = pl.ds(i * 64, 64)
        hi, lo = split(b_ref[0, rows, :])
        bstack[pl.ds(i * 64, 64), :] = hi
        bstack[pl.ds(512 + i * 64, 64), :] = hi
        bstack[pl.ds(1024 + i * 64, 64), :] = lo
        bside[rows, 0:1024] = hi
        bside[rows, 1024:2048] = hi
        bside[rows, 2048:3072] = lo
        for k in range(8):
            plane[k, rows, :] = b_ref[0, rows, k * 128 : k * 128 + 128]
        chi, clo = split(c_ref[i])
        ccat[pl.ds(i * 64, 64), :] = chi
        ccat[pl.ds(512 + i * 64, 64), :] = chi
        ccat[pl.ds(1024 + i * 64, 64), :] = clo

    for i in range(8):
        for p in range(2):
            for k in range(8):
                bperm[pl.ds(i * 64 + p * 32, 32), k * 128 : k * 128 + 128] = plane[
                    k, pl.ds(i * 64 + p, 32, stride=2), :
                ]

    lane = lax.broadcasted_iota(jnp.int32, (32, 128), 1)
    left = lane < 64

    def per_direction(d, carry):
        for i in range(8):
            for q in range(4):
                t0 = t_ref[i * 16 + col_ref[2 * q], d]
                t1 = t_ref[i * 16 + col_ref[2 * q + 1], d]
                even = jnp.where(left, t0, pltpu.roll(t1, 64, 1))
                odd = jnp.where(left, pltpu.roll(t0, 64, 1), t1)
                for p, part in ((0, even), (1, odd)):
                    hi, lo = split(part)
                    rows = pl.ds(i * 64 + p * 32, 32)
                    dcat[rows, q * 128 : q * 128 + 128] = hi
                    dcat[rows, 512 + q * 128 : 640 + q * 128] = lo
                    dcat[rows, 1024 + q * 128 : 1152 + q * 128] = hi
        for n in range(4):
            cols = slice(n * 256, n * 256 + 256)
            projected = dot(dcat[...], bstack[:, cols])
            response = jnp.sum(bperm[:, cols] * projected, axis=0, keepdims=True)
            potential = xc_ref[:, cols] * response + gc_ref[d, :, cols]
            pot[:, cols] = gw_ref[:, cols] * potential
        for i in range(8):
            rows = pl.ds(i * 64, 64)
            hi, lo = split(b_ref[0, rows, :] * pot[...])
            acat[rows, 0:1024] = hi
            acat[rows, 1024:2048] = lo
            acat[rows, 2048:3072] = hi
        for n in range(2):
            ham = dot_nt(acat[...], bside[n * 256 : n * 256 + 256, :])
            for i in range(8):
                part = ham[i * 64 : i * 64 + 64] * mask_ref[i : i + 1, n * 256 : n * 256 + 256]
                hi, lo = split(part)
                rows = pl.ds(i * 64, 64)
                hcat[rows, n * 256 : n * 256 + 256] = hi
                hcat[rows, 512 + n * 256 : 768 + n * 256] = lo
                hcat[rows, 1024 + n * 256 : 1280 + n * 256] = hi
        for n in range(2):
            product = dot(hcat[...], ccat[:, n * 256 : n * 256 + 256])
            for i in range(8):
                for g in range(4):
                    for q in range(2):
                        row = i * 64 + g * 16
                        out_ref[i * 16 + g * 4 + n * 2 + q, d] = product[
                            row : row + 16, q * 128 : q * 128 + 128
                        ]
        return carry

    lax.fori_loop(0, 3, per_direction, 0)


def batch_product(col, mask, tiles, basis, weight, kernel, coord, c_batch):
    return pl.pallas_call(
        batch_kernel,
        out_shape=jax.ShapeDtypeStruct((128, 3, 16, 128), F32),
        in_specs=[smem()] + [vmem()] * 7,
        out_specs=vmem(),
        scratch_shapes=[
            pltpu.VMEM((512, 1024), F32),
            pltpu.VMEM((8, 512, 128), F32),
            pltpu.VMEM((1536, 1024), BF16),
            pltpu.VMEM((512, 3072), BF16),
            pltpu.VMEM((512, 1536), BF16),
            pltpu.VMEM((512, 3072), BF16),
            pltpu.VMEM((512, 1536), BF16),
            pltpu.VMEM((1536, 512), BF16),
            pltpu.VMEM((1, 1024), F32),
        ],
        name="batch_product",
    )(col, mask, tiles, basis, weight, kernel, coord, c_batch)


def solve_kernel(place_ref, arrived_ref, diag_ref, energy_ref, out_ref):
    out_ref[...] = jnp.zeros_like(out_ref)

    def body(b, carry):
        place = place_ref[b]
        out_ref[place] = out_ref[place] + arrived_ref[b]
        return carry

    lax.fori_loop(0, arrived_ref.shape[0], body, 0)
    for k in range(out_ref.shape[0]):
        denominator = diag_ref[k] - energy_ref[...]
        out_ref[k] = -out_ref[k] / denominator[None]


def solve(place, arrived, diag, energy):
    return pl.pallas_call(
        solve_kernel,
        out_shape=jax.ShapeDtypeStruct((16, 3, 16, 128), F32),
        in_specs=[smem()] + [vmem()] * 3,
        out_specs=vmem(),
        name="solve",
    )(place, arrived, diag, energy)


def renew_kernel(
    row_ref, col_ref, xr_ref, xc_ref, cr_ref, cc_ref, out_ref,
    ccat, xccat, xrcat, crcat, dense,
):
    for k in range(8):
        rows = pl.ds(k * 64, 64)
        hi, lo = split(cc_ref[k])
        ccat[rows, 0:512] = hi
        ccat[rows, 512:1024] = hi
        ccat[rows, 1024:1536] = lo
    for k in range(16):
        rows = pl.ds(k * 64, 64)
        hi, lo = split(cr_ref[k])
        crcat[rows, 0:512] = hi
        crcat[rows, 512:1024] = lo
        crcat[rows, 1024:1536] = hi
    lane = lax.broadcasted_iota(jnp.int32, (32, 128), 1)
    left = lane < 64

    def per_direction(d, carry):
        for k in range(8):
            rows = pl.ds(k * 64, 64)
            hi, lo = split(xc_ref[k, d])
            xccat[rows, 0:512] = hi
            xccat[rows, 512:1024] = hi
            xccat[rows, 1024:1536] = lo
        for k in range(16):
            rows = pl.ds(k * 64, 64)
            hi, lo = split(xr_ref[k, d])
            xrcat[rows, 0:512] = hi
            xrcat[rows, 512:1024] = lo
            xrcat[rows, 1024:1536] = hi
        for m in range(4):
            rows = slice(m * 256, m * 256 + 256)
            for n in range(2):
                cols = slice(n * 256, n * 256 + 256)
                value = dot_nt(xrcat[rows, :], ccat[cols, :]) + dot_nt(
                    crcat[rows, :], xccat[cols, :]
                )
                dense[2 * n, rows, :] = value[:, 0:128]
                dense[2 * n + 1, rows, :] = value[:, 128:256]

        def per_slot(s, inner):
            col = col_ref[s]
            start = pl.multiple_of(row_ref[s] * 64, 64)
            half = col % 2
            even = dense[col // 2, pl.ds(start, 32, stride=2), :]
            odd = dense[col // 2, pl.ds(start + 1, 32, stride=2), :]
            even = jnp.where(half == 0, even, pltpu.roll(even, 64, 1))
            odd = jnp.where(half == 1, odd, pltpu.roll(odd, 64, 1))
            out_ref[d, s] = jnp.where(left, even, odd)
            return inner

        lax.fori_loop(0, 32, per_slot, 0)
        return carry

    lax.fori_loop(0, 3, per_direction, 0)


def renew(rows, cols, x_rows, x_cols, c_rows, c_cols):
    return pl.pallas_call(
        renew_kernel,
        out_shape=jax.ShapeDtypeStruct((3, 32, 32, 128), F32),
        in_specs=[smem()] * 2 + [vmem()] * 4,
        out_specs=vmem(),
        scratch_shapes=[
            pltpu.VMEM((512, 1536), BF16),
            pltpu.VMEM((512, 1536), BF16),
            pltpu.VMEM((1024, 1536), BF16),
            pltpu.VMEM((1024, 1536), BF16),
            pltpu.VMEM((4, 1024, 128), F32),
        ],
        name="renew",
    )(rows, cols, x_rows, x_cols, c_rows, c_cols)


def local(
    density_tiles,
    tile_ids,
    batch_blocks,
    basis_values,
    grid_weight,
    xc_kernel,
    grid_coord,
    orbitals,
    precond_diag,
    orbital_energy,
):
    row = lax.axis_index("row")
    col = lax.axis_index("col")
    me = row * 16 + col
    blocks = lax.dynamic_slice_in_dim(batch_blocks, me, 1, 0)[0]

    c_rows = orbitals.reshape(16, TILE, 512)
    asked = lax.dynamic_index_in_dim(batch_blocks.reshape(8, 16, 8), col, 1, keepdims=False)
    asked = lax.dynamic_index_in_dim(asked, row, 1, keepdims=False) - row * 16
    c_batch = lax.all_to_all(
        jnp.take(c_rows, asked, axis=0), "row", split_axis=0, concat_axis=0, tiled=True
    )
    piece = lax.dynamic_slice_in_dim(c_rows, (col % 2) * 8, 8, 0)
    c_cols = lax.psum(jnp.where(row == col // 2, piece, 0.0), "row")

    all_ids = lax.all_gather(tile_ids, ("row", "col"), tiled=True)
    wanted = (blocks[:, None] * NBLK + blocks[None, :]).reshape(-1)
    listed = jnp.any(wanted[:, None] == all_ids[None, :], axis=1).astype(F32).reshape(8, 8)
    mask = jnp.repeat(listed, TILE, axis=1)

    ask_row = lax.dynamic_index_in_dim(batch_blocks, row, 1, keepdims=False)
    ask_col = lax.dynamic_index_in_dim(batch_blocks, col // 2, 1, keepdims=False)
    match = (ask_row * NBLK + ask_col)[:, None] == tile_ids[None, :]
    slots = jnp.max(jnp.where(match, jnp.arange(32, dtype=jnp.int32)[None, :], -1), axis=1)
    outgoing = select_tiles(slots, density_tiles.reshape(3, 32, 32, 128))
    arrived = lax.all_to_all(outgoing, ("row", "col"), split_axis=0, concat_axis=0, tiled=True)

    product = batch_product(
        blocks // 8, mask, arrived, basis_values, grid_weight, xc_kernel, grid_coord, c_batch
    )
    spread = lax.all_to_all(product, ("row", "col"), split_axis=0, concat_axis=0, tiled=True)
    diag = lax.dynamic_index_in_dim(precond_diag.reshape(16, 4, 16), col // 4, 1, keepdims=False)
    energy = lax.dynamic_index_in_dim(orbital_energy.reshape(4, 128), col % 4, 0, keepdims=True)
    x_part = solve(
        ask_row - row * 16, spread, jnp.broadcast_to(diag[:, :, None], (16, 16, 128)), energy
    )
    x_all = lax.all_gather(x_part, "col").reshape(4, 4, 16, 3, 16, 128)
    x_rows = x_all.transpose(2, 3, 0, 4, 1, 5).reshape(16, 3, TILE, 512)
    x_piece = lax.dynamic_slice_in_dim(x_rows, (col % 2) * 8, 8, 0)
    x_cols = lax.psum(jnp.where(row == col // 2, x_piece, 0.0), "row")

    renewed = renew(
        tile_ids // NBLK - row * 16, tile_ids % NBLK - col * 8, x_rows, x_cols, c_rows, c_cols
    )
    return renewed.reshape(3, 32, TILE * TILE)


def solution(mesh):
    placed = (
        P(None, ("row", "col"), None),
        P(("row", "col")),
        P(),
        P(("row", "col"), None, None),
        P(("row", "col"), None),
        P(("row", "col"), None),
        P(None, ("row", "col"), None),
        P("row", None),
        P("row"),
        P(),
    )
    return jax.shard_map(
        local, mesh=mesh, in_specs=placed, out_specs=P(None, ("row", "col"), None), check_vma=False
    )
```

time: 694 us -> 431 us (0.62); the launches traced: 685 us -> 430 us
  waiting for transfers between devices: 377 us -> 172 us
  blocking collectives: 0 us -> 129 us
  local copies, waits for them, and re-layouts: 146 us -> 29.2 us
  matrix products: 97.3 us -> 0 us
  Pallas kernels: 0 us -> 53.4 us
  other arithmetic: 27.9 us -> 10.4 us
    all_to_all x2 -> x3, waiting for transfers between devices: 205 us -> 46.3 us  [the longest x1 39.4 us: local(): lax.all_to_all(product, ('row', 'col'), split_axis=0, concat_axis=0, tile...]
    unnamed x0 -> x1, blocking collectives: none -> 129 us
    psum x3 -> x1, waiting for transfers between devices: 172 us -> 70 us  [local(): x_cols = lax.psum(jnp.where(row == col // 2, x_piece, 0.0), 'row')]
    dot_general x8 -> x0, matrix products: 97.3 us -> none  [the longest x1 15.5 us: local(): jnp.einsum('rs,cs,dsab->dracb', row_hot, col_hot, ham_listed.reshape(3, t...]
    gather x11 -> x1, local copies, waits for them, and re-layouts: 59.3 us -> 2.32 us  [local(): jnp.take(c_rows, asked, axis=0)]
    all_gather x0 -> x1, waiting for transfers between devices: none -> 55.9 us  [local(): x_all = lax.all_gather(x_part, 'col').reshape(4, 4, 16, 3, 16, 128)]
    pallas_call x0 -> x4, Pallas kernels: none -> 53.4 us  [the longest x1 24 us: renew(): pl.pallas_call(renew_kernel, out_shape=jax.ShapeDtypeStruct((3, 32, 32, 1...]
    transpose x3 -> x0, local copies, waits for them, and re-layouts: 32 us -> none  [the longest x1 16.3 us: local(): jnp.einsum('rs,cs,dsab->dracb', row_hot, col_hot, ham_listed.reshape(3, t...]
  transfers between devices with their start and end apart: 5 -> 5, of which waited for: 4 -> 4; matrix products, arithmetic and copies ran while one was open for 11% -> 2% of each run, Pallas kernels for 0% -> 1%
where the time goes in v1:
time: 431 us; the launch traced here: 430 us
  waiting for transfers between devices  172 us (40%)
  blocking collectives  129 us (30%)
  Pallas kernels  53.4 us (12%)
  local copies, waits for them, and re-layouts  29.2 us (7%)
  starting transfers between devices  21.7 us (5%)
  between operations  13.6 us (3%)
  other arithmetic  10.4 us (2%)
    unnamed x1, blocking collectives  129 us
    psum x1, waiting for transfers between devices, local(): x_cols = lax.psum(jnp.where(row == col // 2, x_piece, 0.0), 'row')  70 us
    all_gather x1, waiting for transfers between devices, local(): x_all = lax.all_gather(x_part, 'col').reshape(4, 4, 16, 3, 16, 128)  55.9 us
    all_to_all x1, waiting for transfers between devices, local(): lax.all_to_all(product, ('row', 'col'), split_axis=0, concat_axis=0, tile...  39.4 us
    pallas_call x1, Pallas kernels, renew(): pl.pallas_call(renew_kernel, out_shape=jax.ShapeDtypeStruct((3, 32, 32, 1...  24 us
    pallas_call x1, Pallas kernels, batch_product(): pl.pallas_call(batch_kernel, out_shape=jax.ShapeDtypeStruct((128, 3, 16,...  20 us
    all_to_all x1, starting transfers between devices, local(): lax.all_to_all(outgoing, ('row', 'col'), split_axis=0, concat_axis=0, til...  9.51 us
    reshape x1, local copies, waits for them, and re-layouts, local(): x_all = lax.all_gather(x_part, 'col').reshape(4, 4, 16, 3, 16, 128)  9.47 us
  transfers between devices with their start and end apart: 5, of which 4 were waited for; matrix products, arithmetic and copies ran while one was open for 2% of the time, Pallas kernels for 1%

profile of v1, /device:TPU:1, one launch (start us, length us, event | category | flops | bytes accessed | tf_op | source)
XLA Modules:
  0.0 429.7 jit_solution(9134097311500882792)
XLA Ops:
  6.5 0.8 reshape.91
  7.5 2.3 gather_fusion
  9.8 1.2 broadcast_select_fusion
  11.1 5.9 %all-to-all-start.1 = ((f32[8,64,512]{2,1,0:T(8,128)}), f32[8,64,512]{2,1,0:T(8,128)S(1)}, u32[]{:S(2)}, u32[]{:S(2)}) async-start(f32[8,64,512]{2,1,0:T(8,128)} %broadcast_select_fusion), calls=%async_computation.1 | async-start | bytes 2097152 | tf_op jit(solution)/shard_map/all_to_all | solution.py:279
  17.0 1.4 copy.20
  19.6 5.5 %select_tiles.1 = f32[128,3,32,128]{3,2,1,0:T(8,128)} custom-call(s32[128]{0:T(128)} %select_reduce_fusion.slot_ref, f32[3,32,32,128]{3,2,1,0:T(8,128)} %bitcast.31), custom_call_target="tpu_custom_call" | custom-call | tf_op jit(solution)/shard_map/select_tiles/pallas_call | solution.py:51
  25.0 6.9 %all-to-all-done.1.c_ref = f32[8,64,512]{2,1,0:T(8,128)S(1)} async-done(((f32[8,64,512]{2,1,0:T(8,128)}), f32[8,64,512]{2,1,0:T(8,128)S(1)}, u32[]{:S(2)}, u32[]{:S(2)}) %all-to-all-start.1) | async-done | bytes 1048608 | tf_op jit(solution)/shard_map/all_to_all | solution.py:279
  31.9 1.0 copy-done.2
  32.9 9.5 %all-to-all-start = ((f32[128,3,32,128]{3,2,1,0:T(8,128)}), f32[128,3,32,128]{3,2,1,0:T(8,128)}, u32[]{:S(2)}, u32[]{:S(2)}) async-start(f32[128,3,32,128]{3,2,1,0:T(8,128)} %select_tiles.1), calls=%async_computation | async-start | bytes 12582912 | tf_op jit(solution)/shard_map/all_to_all | solution.py:295
  43.6 129.3 %all-reduce = s32[4096]{0:T(1024)S(1)} all-reduce(s32[4096]{0:T(1024)S(1)} %dynamic-update-slice), channel_id=1, replica_groups=mesh['row'=8,'col'=16] {'row','col'}, use_global_device_ids=true, to_apply=%add | all-reduce | flops 4096 | bytes 32768
  174.0 20.0 %batch_product.1 = f32[128,3,16,128]{3,2,1,0:T(8,128)} custom-call(s32[8]{0:T(128)} %get-tuple-element.10.col_ref, f32[8,512]{1,0:T(8,128)} %reshape.89.mask_ref, f32[128,3,32,128]{3,2,1,0:T(8,128)} %all-to-all-done.t_ref, f32[1,512,1024]{2,1,0:T(8,128)} %b_ref.1, f32[1,1024]{1,0:T(1,128)} %gw_ref.1, f32[1,1024]{1,0:T(1,128)} %xc_ref.1, ...), custom_call_target="tpu_custom_call" | custom-call | tf_op jit(solution)/shard_map/batch_product/pallas_call | solution.py:139
  194.0 6.0 %all-to-all-start.2 = ((f32[128,3,16,128]{3,2,1,0:T(8,128)}), f32[128,3,16,128]{3,2,1,0:T(8,128)S(1)}, u32[]{:S(2)}, u32[]{:S(2)}) async-start(f32[128,3,16,128]{3,2,1,0:T(8,128)} %batch_product.1), calls=%async_computation.2 | async-start | bytes 6291456 | tf_op jit(solution)/shard_map/all_to_all | solution.py:300
  200.8 39.4 %all-to-all-done.2.arrived_ref = f32[128,3,16,128]{3,2,1,0:T(8,128)S(1)} async-done(((f32[128,3,16,128]{3,2,1,0:T(8,128)}), f32[128,3,16,128]{3,2,1,0:T(8,128)S(1)}, u32[]{:S(2)}, u32[]{:S(2)}) %all-to-all-start.2) | async-done | bytes 3145760 | tf_op jit(solution)/shard_map/all_to_all | solution.py:300
  240.2 0.9 broadcast_in_dim.51.diag_ref
  241.0 0.8 copy-done.1
  241.9 3.9 solve.1
  246.0 2.3 dynamic-slice_select_fusion.1
  248.3 55.9 %all-gather.3.cloned.1.call-done = f32[256,3,16,128]{3,2,1,0:T(8,128)} async-done(((f32[16,3,16,128]{3,2,1,0:T(8,128)}), f32[256,3,16,128]{3,2,1,0:T(8,128)}) %all-gather.3.cloned.1.call-update) | async-done | bytes 6291472 | tf_op jit(solution)/shard_map/all_gather | solution.py:306
  304.2 9.5 %copy.23 = f32[4,4,16,3,16,128]{5,1,4,0,3,2:T(4,128)} copy(f32[4,4,16,3,16,128]{5,4,3,2,1,0:T(8,128)} %bitcast.30) | data formatting | bytes 12582912 | tf_op jit(solution)/shard_map/reshape | solution.py:306
  313.7 7.9 %reshape.96.xr_ref = f32[16,3,64,512]{3,2,1,0:T(8,128)} reshape(f32[16,3,4,16,4,128]{5,4,3,2,1,0:T(4,128)} %bitcast.26) | data formatting | bytes 12582912 | tf_op jit(solution)/shard_map/reshape | solution.py:307
  321.6 4.1 dynamic-slice_select_fusion
  326.3 70.0 %all-reduce.4.cloned.1.call-done = (f32[8,3,64,512]{3,2,1,0:T(8,128)}, f32[8,64,512]{2,1,0:T(8,128)}) async-done(((f32[8,3,64,512]{3,2,1,0:T(8,128)}, f32[8,64,512]{2,1,0:T(8,128)}), (f32[8,3,64,512]{3,2,1,0:T(8,128)}, f32[8,64,512]{2,1,0:T(8,128)})) %all-reduce.4.cloned.1.call-update) | async-done | bytes 4194320 | tf_op jit(solution)/shard_map/psum | solution.py:309
  396.3 24.0 %renew.1 = f32[3,32,32,128]{3,2,1,0:T(8,128)} custom-call(s32[32]{0:T(128)} %get-tuple-element.12.row_ref, s32[32]{0:T(128)} %get-tuple-element.11.col_ref, f32[16,3,64,512]{3,2,1,0:T(8,128)} %reshape.96.xr_ref, f32[8,3,64,512]{3,2,1,0:T(8,128)} %get-tuple-element.5.xc_ref, f32[16,64,512]{2,1,0:T(8,128)} %bitcast.29, f32[8,64,512]{2,1,0:T(8,128)} %get-tuple-element.6.cc_ref), custom_call_target="tpu_custom_call" | custom-call | tf_op jit(solution)/shard_map/renew/pallas_call | solution.py:243
  420.3 2.6 reshape.97
  (39 shorter events, 5.2 us)
Async XLA Ops:
  6.5 193.6 %copy-start = (f32[512]{0:T(512)S(1)}, f32[512]{0:T(512)}, u32[]{:S(2)}) copy-start(f32[512]{0:T(512)} %param.19) | copy-start | bytes 6148
  7.5 9.5 %copy-start.3 = (f32[3,32,4096]{2,1,0:T(8,128)S(1)}, f32[3,32,4096]{2,1,0:T(8,128)}, u32[]{:S(2)}) copy-start(f32[3,32,4096]{2,1,0:T(8,128)} %param.10) | copy-start | bytes 4718596
  11.0 7.3 %copy-start.4 = (s32[128,8]{0,1:T(8,128)S(1)}, s32[128,8]{0,1:T(8,128)}, u32[]{:S(2)}) copy-start(s32[128,8]{0,1:T(8,128)} %param.12) | copy-start | bytes 12292
  11.1 7.8 %copy-start.6 = (s32[32]{0:T(128)S(1)}, s32[32]{0:T(128)}, u32[]{:S(2)}) copy-start(s32[32]{0:T(128)} %param.11) | copy-start | bytes 388
  11.1 20.9 %all-to-all-start.1 = ((f32[8,64,512]{2,1,0:T(8,128)}), f32[8,64,512]{2,1,0:T(8,128)S(1)}, u32[]{:S(2)}, u32[]{:S(2)}) async-start(f32[8,64,512]{2,1,0:T(8,128)} %broadcast_select_fusion), calls=%async_computation.1 | async-start | bytes 2097152 | tf_op jit(solution)/shard_map/all_to_all | solution.py:279
  31.9 1.0 copy-start.2
  32.9 141.1 %all-to-all-start = ((f32[128,3,32,128]{3,2,1,0:T(8,128)}), f32[128,3,32,128]{3,2,1,0:T(8,128)}, u32[]{:S(2)}, u32[]{:S(2)}) async-start(f32[128,3,32,128]{3,2,1,0:T(8,128)} %select_tiles.1), calls=%async_computation | async-start | bytes 12582912 | tf_op jit(solution)/shard_map/all_to_all | solution.py:295
  194.0 6.0 %copy-start.5 = (f32[1024]{0:T(1024)S(1)}, f32[1024]{0:T(1024)}, u32[]{:S(2)}) copy-start(f32[1024]{0:T(1024)} %param.18) | copy-start | bytes 12292
  194.0 46.2 %all-to-all-start.2 = ((f32[128,3,16,128]{3,2,1,0:T(8,128)}), f32[128,3,16,128]{3,2,1,0:T(8,128)S(1)}, u32[]{:S(2)}, u32[]{:S(2)}) async-start(f32[128,3,16,128]{3,2,1,0:T(8,128)} %batch_product.1), calls=%async_computation.2 | async-start | bytes 6291456 | tf_op jit(solution)/shard_map/all_to_all | solution.py:300
  200.0 104.2 %all-gather.3.cloned.1.call-start = ((), (), s32[]{:S(2)}) async-start(), calls=%async_computation.3 | async-start | bytes 6684672 | tf_op jit(solution)/shard_map/all_gather | solution.py:306
  240.2 1.7 copy-start.1
  245.7 150.5 %all-reduce.4.cloned.1.call-start = ((), (), s32[]{:S(2)}) async-start(), calls=%async_computation.4 | async-start | bytes 8388608 | tf_op jit(solution)/shard_map/psum | solution.py:309
Sparse Core Ops, SparseCore 0:
  245.9 58.2 all-gather.2
  325.8 70.4 all-reduce.3

commit v2 on v1

--- a/solution.py
+++ b/solution.py
@@ -39,9 +39,8 @@
 
     def body(n, carry):
         slot = slot_ref[n]
-        found = jnp.where(slot >= 0, 1.0, 0.0).astype(F32)
         picked = tiles_ref[:, jnp.maximum(slot, 0)]
-        out_ref[n] = picked * found
+        out_ref[n] = jnp.where(slot >= 0, picked, jnp.inf)
         return carry
 
     lax.fori_loop(0, count, body, 0)
@@ -58,8 +57,8 @@
 
 
 def batch_kernel(
-    col_ref, mask_ref, t_ref, b_ref, gw_ref, xc_ref, gc_ref, c_ref, out_ref,
-    bperm, plane, bstack, bside, dcat, acat, hcat, ccat, pot,
+    col_ref, t_ref, b_ref, gw_ref, xc_ref, gc_ref, c_ref, out_ref,
+    bperm, plane, bstack, bside, dcat, acat, hcat, ccat, pot, mask,
 ):
     for i in range(8):
         rows = pl.ds(i * 64, 64)
@@ -92,6 +91,15 @@
             for q in range(4):
                 t0 = t_ref[i * 16 + col_ref[2 * q], d]
                 t1 = t_ref[i * 16 + col_ref[2 * q + 1], d]
+                listed0 = t0 < jnp.inf
+                listed1 = t1 < jnp.inf
+                t0 = jnp.where(listed0, t0, 0.0)
+                t1 = jnp.where(listed1, t1, 0.0)
+                mask[i : i + 1, q * 128 : q * 128 + 128] = jnp.where(
+                    left[0:1],
+                    jnp.where(listed0[0:1], 1.0, 0.0),
+                    jnp.where(listed1[0:1], 1.0, 0.0),
+                )
                 even = jnp.where(left, t0, pltpu.roll(t1, 64, 1))
                 odd = jnp.where(left, pltpu.roll(t0, 64, 1), t1)
                 for p, part in ((0, even), (1, odd)):
@@ -115,7 +123,7 @@
         for n in range(2):
             ham = dot_nt(acat[...], bside[n * 256 : n * 256 + 256, :])
             for i in range(8):
-                part = ham[i * 64 : i * 64 + 64] * mask_ref[i : i + 1, n * 256 : n * 256 + 256]
+                part = ham[i * 64 : i * 64 + 64] * mask[i : i + 1, n * 256 : n * 256 + 256]
                 hi, lo = split(part)
                 rows = pl.ds(i * 64, 64)
                 hcat[rows, n * 256 : n * 256 + 256] = hi
@@ -135,11 +143,11 @@
     lax.fori_loop(0, 3, per_direction, 0)
 
 
-def batch_product(col, mask, tiles, basis, weight, kernel, coord, c_batch):
+def batch_product(col, tiles, basis, weight, kernel, coord, c_batch):
     return pl.pallas_call(
         batch_kernel,
         out_shape=jax.ShapeDtypeStruct((128, 3, 16, 128), F32),
-        in_specs=[smem()] + [vmem()] * 7,
+        in_specs=[smem()] + [vmem()] * 6,
         out_specs=vmem(),
         scratch_shapes=[
             pltpu.VMEM((512, 1024), F32),
@@ -151,9 +159,10 @@
             pltpu.VMEM((512, 1536), BF16),
             pltpu.VMEM((1536, 512), BF16),
             pltpu.VMEM((1, 1024), F32),
+            pltpu.VMEM((8, 512), F32),
         ],
         name="batch_product",
-    )(col, mask, tiles, basis, weight, kernel, coord, c_batch)
+    )(col, tiles, basis, weight, kernel, coord, c_batch)
 
 
 def solve_kernel(place_ref, arrived_ref, diag_ref, energy_ref, out_ref):
@@ -180,13 +189,256 @@
     )(place, arrived, diag, energy)
 
 
+MESH = pl.DeviceIdType.MESH
+
+
+def spread_kernel(
+    x_ref, c_ref, rows_ref, cols_ref,
+    own_sem, ring_send, ring_recv, scatter_send, scatter_recv, line_send, line_recv,
+):
+    row = lax.axis_index("row")
+    col = lax.axis_index("col")
+    z, y = col // 4, col % 4
+    x, core = row // 2, row % 2
+    home = col // 2 == row
+
+    def across(axis, step):
+        if axis == 0:
+            return (row, lax.rem(z + step + 4, 4) * 4 + y)
+        return (row, z * 4 + lax.rem(y + step + 4, 4))
+
+    def along(step):
+        return (lax.rem(x + step + 4, 4) * 2 + core, col)
+
+    partner = (x * 2 + 1 - core, col)
+
+    barrier = pltpu.get_barrier_semaphore()
+    for device in (
+        across(0, 1), across(0, -1), across(1, 1), across(1, -1), along(1), along(-1), partner
+    ):
+        pl.semaphore_signal(barrier, inc=1, device_id=device, device_id_type=MESH)
+
+    def greet(k, carry):
+        @pl.when(jnp.logical_or(col // 2 != row, k != col))
+        def _():
+            pl.semaphore_signal(barrier, inc=1, device_id=(col // 2, k), device_id_type=MESH)
+
+        return carry
+
+    lax.fori_loop(0, 16, greet, 0)
+    pl.semaphore_wait(barrier, 23 - home.astype(jnp.int32))
+
+    def remote(src, dst, send, recv, device):
+        return pltpu.make_async_remote_copy(
+            src_ref=src, dst_ref=dst, send_sem=send, recv_sem=recv,
+            device_id=device, device_id_type=MESH,
+        )
+
+    def window(ref, block, planes, oz, oy):
+        return ref.at[
+            block, planes,
+            pl.ds(pl.multiple_of(oz * 16, 16), 16), pl.ds(pl.multiple_of(oy * 128, 128), 128),
+        ]
+
+    def scatter(k, h):
+        return remote(
+            x_ref.at[h * 8 + k], window(cols_ref, k, pl.ds(0, 3), z, y),
+            scatter_send.at[h * 8 + k], scatter_recv, (k, row * 2 + h),
+        )
+
+    def scatter_orbitals(k):
+        return remote(
+            c_ref.at[(col % 2) * 8 + k], cols_ref.at[k, 3],
+            scatter_send.at[16 + k], scatter_recv, (k, col),
+        )
+
+    def start_scatter(k, carry):
+        for h in range(2):
+            here = jnp.logical_and(k == row, row * 2 + h == col)
+
+            @pl.when(here)
+            def _():
+                pltpu.make_async_copy(
+                    x_ref.at[h * 8 + k], window(cols_ref, k, pl.ds(0, 3), z, y), scatter_recv
+                ).start()
+
+            @pl.when(jnp.logical_not(here))
+            def _():
+                scatter(k, h).start()
+
+        @pl.when(jnp.logical_and(home, k == row))
+        def _():
+            pltpu.make_async_copy(
+                c_ref.at[(col % 2) * 8 + k], cols_ref.at[k, 3], scatter_recv
+            ).start()
+
+        @pl.when(jnp.logical_and(home, k != row))
+        def _():
+            scatter_orbitals(k).start()
+
+        return carry
+
+    lax.fori_loop(0, 8, start_scatter, 0)
+
+    def spot(half, first, second, blocks):
+        oz, oy = (z + second, y + first) if half == 0 else (z + first, y + second)
+        lo, count = blocks
+        return window(
+            rows_ref, pl.ds(half * 8 + lo, count), pl.ds(0, 3),
+            lax.rem(oz + 8, 4), lax.rem(oy + 8, 4),
+        )
+
+    ALL, LOW, HIGH = (0, 8), (0, 4), (4, 4)
+
+    def hop(half, phase, index, first, second, blocks, step):
+        axis = (1, 0)[half] if phase == 0 else (0, 1)[half]
+        if first == 0 and second == 0:
+            src = x_ref.at[pl.ds(half * 8, 8)]
+        else:
+            src = spot(half, first, second, blocks)
+        return remote(
+            src, spot(half, first, second, blocks),
+            ring_send.at[half, index], ring_recv.at[half, index], across(axis, step),
+        )
+
+    ORIGINS = (0, -1, 1, 2)
+    sent = []
+
+    def go(*args):
+        copy = hop(*args)
+        copy.start()
+        sent.append(copy)
+
+    def arrive(half, phase, index, first, second, blocks):
+        hop(half, phase, index, first, second, blocks, 1).wait_recv()
+
+    own = [
+        pltpu.make_async_copy(
+            x_ref.at[pl.ds(half * 8, 8)], spot(half, 0, 0, ALL), own_sem.at[half]
+        )
+        for half in range(2)
+    ]
+    for half in range(2):
+        go(half, 0, 0, 0, 0, ALL, 1)
+        go(half, 0, 1, 0, 0, ALL, -1)
+    for half in range(2):
+        go(half, 1, 4, 0, 0, ALL, 1)
+        go(half, 1, 5, 0, 0, ALL, -1)
+        own[half].start()
+
+    pltpu.make_async_copy(cols_ref.at[row], cols_ref.at[row], scatter_recv).wait()
+
+    def line(index, distance, planes, device):
+        block = lax.rem(x + distance + 4, 4) * 2 + core
+        ref = cols_ref.at[block, planes]
+        return remote(ref, ref, line_send.at[index], line_recv.at[index], device)
+
+    def landed(index, distance, planes, other):
+        owner = core if other == 0 else 1 - core
+        ref = cols_ref.at[lax.rem(x + distance + 4, 4) * 2 + owner, planes]
+        remote(ref, ref, line_send.at[index], line_recv.at[index], partner).wait_recv()
+
+    FULL, FRONT, BACK = pl.ds(0, 4), pl.ds(0, 2), pl.ds(2, 2)
+    lines = []
+
+    def pass_on(index, distance, planes, device):
+        copy = line(index, distance, planes, device)
+        copy.start()
+        lines.append(copy)
+
+    pass_on(0, 0, FULL, along(1))
+    pass_on(1, 0, FULL, along(-1))
+    pass_on(4, 0, FULL, partner)
+
+    for half in range(2):
+        arrive(half, 0, 0, -1, 0, ALL)
+        go(half, 0, 2, -1, 0, LOW, 1)
+        go(half, 1, 6, -1, 0, ALL, 1)
+        go(half, 1, 7, -1, 0, ALL, -1)
+        arrive(half, 0, 1, 1, 0, ALL)
+        go(half, 0, 3, 1, 0, HIGH, -1)
+        go(half, 1, 8, 1, 0, ALL, 1)
+        go(half, 1, 9, 1, 0, ALL, -1)
+    landed(0, -1, FULL, 0)
+    pass_on(2, -1, FRONT, along(1))
+    pass_on(5, -1, FULL, partner)
+    landed(1, 1, FULL, 0)
+    pass_on(3, 1, BACK, along(-1))
+    pass_on(6, 1, FULL, partner)
+    for half in range(2):
+        arrive(half, 0, 2, 2, 0, LOW)
+        arrive(half, 0, 3, 2, 0, HIGH)
+        go(half, 1, 10, 2, 0, ALL, 1)
+        go(half, 1, 11, 2, 0, ALL, -1)
+    for k, first in enumerate(ORIGINS):
+        for half in range(2):
+            arrive(half, 1, 4 + 2 * k, first, -1, ALL)
+            go(half, 1, 12 + 2 * k, first, -1, LOW, 1)
+            arrive(half, 1, 5 + 2 * k, first, 1, ALL)
+            go(half, 1, 13 + 2 * k, first, 1, HIGH, -1)
+        if k == 1:
+            landed(2, 2, FRONT, 0)
+            landed(3, 2, BACK, 0)
+            pass_on(7, 2, FULL, partner)
+    for k, first in enumerate(ORIGINS):
+        for half in range(2):
+            arrive(half, 1, 12 + 2 * k, first, 2, LOW)
+            arrive(half, 1, 13 + 2 * k, first, 2, HIGH)
+    landed(4, 0, FULL, 1)
+    landed(5, -1, FULL, 1)
+    landed(6, 1, FULL, 1)
+    landed(7, 2, FULL, 1)
+    for copy in own:
+        copy.wait()
+    for copy in sent + lines:
+        copy.wait_send()
+
+    def finish_scatter(k, carry):
+        for h in range(2):
+            @pl.when(jnp.logical_not(jnp.logical_and(k == row, row * 2 + h == col)))
+            def _():
+                scatter(k, h).wait_send()
+
+        @pl.when(jnp.logical_and(home, k != row))
+        def _():
+            scatter_orbitals(k).wait_send()
+
+        return carry
+
+    lax.fori_loop(0, 8, finish_scatter, 0)
+
+
+def spread_orbitals(x_part, c_rows):
+    any_space = pl.BlockSpec(memory_space=pl.ANY)
+    return pl.pallas_call(
+        spread_kernel,
+        out_shape=(
+            jax.ShapeDtypeStruct((16, 3, TILE, 512), F32),
+            jax.ShapeDtypeStruct((8, 4, TILE, 512), F32),
+        ),
+        in_specs=[any_space, any_space],
+        out_specs=(any_space, any_space),
+        scratch_shapes=[
+            pltpu.SemaphoreType.DMA((2,)),
+            pltpu.SemaphoreType.DMA((2, 20)),
+            pltpu.SemaphoreType.DMA((2, 20)),
+            pltpu.SemaphoreType.DMA((24,)),
+            pltpu.SemaphoreType.DMA,
+            pltpu.SemaphoreType.DMA((8,)),
+            pltpu.SemaphoreType.DMA((8,)),
+        ],
+        compiler_params=pltpu.CompilerParams(collective_id=1, has_side_effects=True),
+        name="spread_orbitals",
+    )(x_part, c_rows)
+
+
 def renew_kernel(
-    row_ref, col_ref, xr_ref, xc_ref, cr_ref, cc_ref, out_ref,
+    row_ref, col_ref, xr_ref, xc_ref, cr_ref, out_ref,
     ccat, xccat, xrcat, crcat, dense,
 ):
     for k in range(8):
         rows = pl.ds(k * 64, 64)
-        hi, lo = split(cc_ref[k])
+        hi, lo = split(xc_ref[k, 3])
         ccat[rows, 0:512] = hi
         ccat[rows, 512:1024] = hi
         ccat[rows, 1024:1536] = lo
@@ -239,11 +491,11 @@
     lax.fori_loop(0, 3, per_direction, 0)
 
 
-def renew(rows, cols, x_rows, x_cols, c_rows, c_cols):
+def renew(rows, cols, x_rows, x_cols, c_rows):
     return pl.pallas_call(
         renew_kernel,
         out_shape=jax.ShapeDtypeStruct((3, 32, 32, 128), F32),
-        in_specs=[smem()] * 2 + [vmem()] * 4,
+        in_specs=[smem()] * 2 + [vmem()] * 3,
         out_specs=vmem(),
         scratch_shapes=[
             pltpu.VMEM((512, 1536), BF16),
@@ -253,7 +505,7 @@
             pltpu.VMEM((4, 1024, 128), F32),
         ],
         name="renew",
-    )(rows, cols, x_rows, x_cols, c_rows, c_cols)
+    )(rows, cols, x_rows, x_cols, c_rows)
 
 
 def local(
@@ -279,14 +531,6 @@
     c_batch = lax.all_to_all(
         jnp.take(c_rows, asked, axis=0), "row", split_axis=0, concat_axis=0, tiled=True
     )
-    piece = lax.dynamic_slice_in_dim(c_rows, (col % 2) * 8, 8, 0)
-    c_cols = lax.psum(jnp.where(row == col // 2, piece, 0.0), "row")
-
-    all_ids = lax.all_gather(tile_ids, ("row", "col"), tiled=True)
-    wanted = (blocks[:, None] * NBLK + blocks[None, :]).reshape(-1)
-    listed = jnp.any(wanted[:, None] == all_ids[None, :], axis=1).astype(F32).reshape(8, 8)
-    mask = jnp.repeat(listed, TILE, axis=1)
-
     ask_row = lax.dynamic_index_in_dim(batch_blocks, row, 1, keepdims=False)
     ask_col = lax.dynamic_index_in_dim(batch_blocks, col // 2, 1, keepdims=False)
     match = (ask_row * NBLK + ask_col)[:, None] == tile_ids[None, :]
@@ -295,7 +539,7 @@
     arrived = lax.all_to_all(outgoing, ("row", "col"), split_axis=0, concat_axis=0, tiled=True)
 
     product = batch_product(
-        blocks // 8, mask, arrived, basis_values, grid_weight, xc_kernel, grid_coord, c_batch
+        blocks // 8, arrived, basis_values, grid_weight, xc_kernel, grid_coord, c_batch
     )
     spread = lax.all_to_all(product, ("row", "col"), split_axis=0, concat_axis=0, tiled=True)
     diag = lax.dynamic_index_in_dim(precond_diag.reshape(16, 4, 16), col // 4, 1, keepdims=False)
@@ -303,14 +547,8 @@
     x_part = solve(
         ask_row - row * 16, spread, jnp.broadcast_to(diag[:, :, None], (16, 16, 128)), energy
     )
-    x_all = lax.all_gather(x_part, "col").reshape(4, 4, 16, 3, 16, 128)
-    x_rows = x_all.transpose(2, 3, 0, 4, 1, 5).reshape(16, 3, TILE, 512)
-    x_piece = lax.dynamic_slice_in_dim(x_rows, (col % 2) * 8, 8, 0)
-    x_cols = lax.psum(jnp.where(row == col // 2, x_piece, 0.0), "row")
-
-    renewed = renew(
-        tile_ids // NBLK - row * 16, tile_ids % NBLK - col * 8, x_rows, x_cols, c_rows, c_cols
-    )
+    x_rows, cols = spread_orbitals(x_part, c_rows)
+    renewed = renew(tile_ids // NBLK - row * 16, tile_ids % NBLK - col * 8, x_rows, cols, c_rows)
     return renewed.reshape(3, 32, TILE * TILE)
 
 

time: 431 us -> 259 us (0.60)
  blocking collectives: 129 us -> 0 us
  waiting for transfers between devices: 172 us -> 121 us
  Pallas kernels: 53.4 us -> 99.6 us
  local copies, waits for them, and re-layouts: 29.2 us -> 10.5 us
  between operations: 13.6 us -> 0.13 us
  other arithmetic: 10.4 us -> 3.57 us
    unnamed x1 -> x0, blocking collectives: 129 us -> none
    all_to_all x1, waiting for transfers between devices: 0.01 us -> 75.2 us  [local(): lax.all_to_all(outgoing, ('row', 'col'), split_axis=0, concat_axis=0, til...]
    psum x1 -> x0, waiting for transfers between devices: 70 us -> none  [local(): x_cols = lax.psum(jnp.where(row == col // 2, x_piece, 0.0), 'row')]
    all_gather x1 -> x0, waiting for transfers between devices: 55.9 us -> none  [local(): x_all = lax.all_gather(x_part, 'col').reshape(4, 4, 16, 3, 16, 128)]
    pallas_call x0 -> x1, Pallas kernels: none -> 45.9 us  [spread_orbitals(): pl.pallas_call(spread_kernel, out_shape=(jax.ShapeDtypeStruct((16, 3, TIL...]
    reshape x3 -> x0, local copies, waits for them, and re-layouts: 18 us -> none  [the longest x1 9.47 us: local(): x_all = lax.all_gather(x_part, 'col').reshape(4, 4, 16, 3, 16, 128)]
    select_n x2 -> x1, other arithmetic: 6.41 us -> 0.53 us  [local(): blocks // 8]
  transfers between devices with their start and end apart: 5 -> 3, of which waited for: 4 -> 3; matrix products, arithmetic and copies ran while one was open for 2% -> 2% of each run, Pallas kernels for 1% -> 2%
where the time goes in v2:
time: 259 us; the launch traced here: 258 us
  waiting for transfers between devices  121 us (47%)
  Pallas kernels  99.6 us (38%)
  starting transfers between devices  23.5 us (9%)
  local copies, waits for them, and re-layouts  10.5 us (4%)
  other arithmetic  3.57 us (1%)
    all_to_all x1, waiting for transfers between devices, local(): lax.all_to_all(outgoing, ('row', 'col'), split_axis=0, concat_axis=0, til...  75.2 us
    pallas_call x1, Pallas kernels, spread_orbitals(): pl.pallas_call(spread_kernel, out_shape=(jax.ShapeDtypeStruct((16, 3, TIL...  45.9 us
    all_to_all x1, waiting for transfers between devices, local(): lax.all_to_all(product, ('row', 'col'), split_axis=0, concat_axis=0, tile...  39 us
    pallas_call x1, Pallas kernels, renew(): pl.pallas_call(renew_kernel, out_shape=jax.ShapeDtypeStruct((3, 32, 32, 1...  24.1 us
    pallas_call x1, Pallas kernels, batch_product(): pl.pallas_call(batch_kernel, out_shape=jax.ShapeDtypeStruct((128, 3, 16,...  20 us
    all_to_all x1, starting transfers between devices, local(): lax.all_to_all(outgoing, ('row', 'col'), split_axis=0, concat_axis=0, til...  9.51 us
    all_to_all x1, starting transfers between devices, local(): lax.all_to_all(product, ('row', 'col'), split_axis=0, concat_axis=0, tile...  8.19 us
    all_to_all x1, waiting for transfers between devices, local(): lax.all_to_all(jnp.take(c_rows, asked, axis=0), 'row', split_axis=0, conc...  6.72 us
  transfers between devices with their start and end apart: 3, of which 3 were waited for; matrix products, arithmetic and copies ran while one was open for 2% of the time, Pallas kernels for 2%

profile of v2, /device:TPU:1, one launch (start us, length us, event | category | flops | bytes accessed | tf_op | source)
XLA Modules:
  0.0 258.3 jit_solution(8938517948504656943)
XLA Ops:
  0.0 0.8 reshape.55
  1.0 2.2 gather_fusion
  3.2 1.2 broadcast_select_fusion
  4.4 5.8 %all-to-all-start.1 = ((f32[8,64,512]{2,1,0:T(8,128)}), f32[8,64,512]{2,1,0:T(8,128)S(1)}, u32[]{:S(2)}, u32[]{:S(2)}) async-start(f32[8,64,512]{2,1,0:T(8,128)} %broadcast_select_fusion), calls=%async_computation.1 | async-start | bytes 2097152 | tf_op jit(solution)/shard_map/all_to_all | solution.py:531
  10.2 1.4 copy.15
  11.6 0.5 fusion.1
  12.1 0.6 select_reduce_fusion.slot_ref
  12.7 5.7 %select_tiles.1 = f32[128,3,32,128]{3,2,1,0:T(8,128)} custom-call(s32[128]{0:T(128)} %select_reduce_fusion.slot_ref, f32[3,32,32,128]{3,2,1,0:T(8,128)} %bitcast.25), custom_call_target="tpu_custom_call" | custom-call | tf_op jit(solution)/shard_map/select_tiles/pallas_call | solution.py:50
  18.4 6.7 %all-to-all-done.1.c_ref = f32[8,64,512]{2,1,0:T(8,128)S(1)} async-done(((f32[8,64,512]{2,1,0:T(8,128)}), f32[8,64,512]{2,1,0:T(8,128)S(1)}, u32[]{:S(2)}, u32[]{:S(2)}) %all-to-all-start.1) | async-done | bytes 1048608 | tf_op jit(solution)/shard_map/all_to_all | solution.py:531
  25.2 1.0 copy-done.2
  26.1 9.5 %all-to-all-start = ((f32[128,3,32,128]{3,2,1,0:T(8,128)}), f32[128,3,32,128]{3,2,1,0:T(8,128)}, u32[]{:S(2)}, u32[]{:S(2)}) async-start(f32[128,3,32,128]{3,2,1,0:T(8,128)} %select_tiles.1), calls=%async_computation | async-start | bytes 12582912 | tf_op jit(solution)/shard_map/all_to_all | solution.py:539
  35.8 0.5 and_select_fusion.col_ref
  36.4 75.2 %all-to-all-done.t_ref = f32[128,3,32,128]{3,2,1,0:T(8,128)} async-done(((f32[128,3,32,128]{3,2,1,0:T(8,128)}), f32[128,3,32,128]{3,2,1,0:T(8,128)}, u32[]{:S(2)}, u32[]{:S(2)}) %all-to-all-start) | async-done | bytes 6291488 | tf_op jit(solution)/shard_map/all_to_all | solution.py:539
  111.6 20.0 %batch_product.1 = f32[128,3,16,128]{3,2,1,0:T(8,128)} custom-call(s32[8]{0:T(128)} %and_select_fusion.col_ref, f32[128,3,32,128]{3,2,1,0:T(8,128)} %all-to-all-done.t_ref, f32[1,512,1024]{2,1,0:T(8,128)} %b_ref.1, f32[1,1024]{1,0:T(1,128)} %gw_ref.1, f32[1,1024]{1,0:T(1,128)} %xc_ref.1, f32[3,1,1024]{2,1,0:T(1,128)} %gc_ref.1, f32[8,64,512]{2,1,0:T(8,128)} %copy-done.2), custom_call_target="tpu_custom_call" | custom-call | tf_op jit(solution)/shard_map/batch_product/pallas_call | solution.py:147
  131.6 8.2 %all-to-all-start.2 = ((f32[128,3,16,128]{3,2,1,0:T(8,128)}), f32[128,3,16,128]{3,2,1,0:T(8,128)S(1)}, u32[]{:S(2)}, u32[]{:S(2)}) async-start(f32[128,3,16,128]{3,2,1,0:T(8,128)} %batch_product.1), calls=%async_computation.2 | async-start | bytes 6291456 | tf_op jit(solution)/shard_map/all_to_all | solution.py:544
  140.0 0.6 constant_dynamic-slice_fusion.energy_ref
  140.6 0.6 fusion.2
  141.2 39.0 %all-to-all-done.2.arrived_ref = f32[128,3,16,128]{3,2,1,0:T(8,128)S(1)} async-done(((f32[128,3,16,128]{3,2,1,0:T(8,128)}), f32[128,3,16,128]{3,2,1,0:T(8,128)S(1)}, u32[]{:S(2)}, u32[]{:S(2)}) %all-to-all-start.2) | async-done | bytes 3145760 | tf_op jit(solution)/shard_map/all_to_all | solution.py:544
  180.2 0.9 broadcast_in_dim.38.diag_ref
  181.1 0.8 copy-done.1
  181.8 3.9 %solve.1.x_ref = f32[16,3,16,128]{3,2,1,0:T(8,128)} custom-call(s32[128]{0:T(128)} %get-tuple-element.10.place_ref, f32[128,3,16,128]{3,2,1,0:T(8,128)} %copy-done.1, f32[16,16,128]{2,1,0:T(8,128)} %broadcast_in_dim.38.diag_ref, f32[1,128]{1,0:T(1,128)} %constant_dynamic-slice_fusion.energy_ref), custom_call_target="tpu_custom_call" | custom-call | tf_op jit(solution)/shard_map/solve/pallas_call | solution.py:183
  185.7 45.9 %spread_orbitals.1 = (f32[16,3,64,512]{3,2,1,0:T(8,128)}, f32[8,4,64,512]{3,2,1,0:T(8,128)}) custom-call(f32[16,3,16,128]{3,2,1,0:T(8,128)} %solve.1.x_ref, f32[16,64,512]{2,1,0:T(8,128)} %bitcast.23), custom_call_target="tpu_custom_call" | custom-call | tf_op jit(solution)/shard_map/spread_orbitals/pallas_call | solution.py:413
  231.6 24.1 %renew.1 = f32[3,32,32,128]{3,2,1,0:T(8,128)} custom-call(s32[32]{0:T(128)} %get-tuple-element.12.row_ref, s32[32]{0:T(128)} %get-tuple-element.11.col_ref, f32[16,3,64,512]{3,2,1,0:T(8,128)} %get-tuple-element.7.xr_ref, f32[8,4,64,512]{3,2,1,0:T(8,128)} %get-tuple-element.8.xc_ref, f32[16,64,512]{2,1,0:T(8,128)} %bitcast.24), custom_call_target="tpu_custom_call" | custom-call | tf_op jit(solution)/shard_map/renew/pallas_call | solution.py:495
  255.7 2.6 reshape.59
  (20 shorter events, 0.5 us)
Async XLA Ops:
  0.0 140.0 %copy-start = (f32[512]{0:T(512)S(1)}, f32[512]{0:T(512)}, u32[]{:S(2)}) copy-start(f32[512]{0:T(512)} %param.19) | copy-start | bytes 6148
  3.2 7.0 %copy-start.3 = (f32[3,32,4096]{2,1,0:T(8,128)S(1)}, f32[3,32,4096]{2,1,0:T(8,128)}, u32[]{:S(2)}) copy-start(f32[3,32,4096]{2,1,0:T(8,128)} %param.10) | copy-start | bytes 4718596
  4.4 20.8 %all-to-all-start.1 = ((f32[8,64,512]{2,1,0:T(8,128)}), f32[8,64,512]{2,1,0:T(8,128)S(1)}, u32[]{:S(2)}, u32[]{:S(2)}) async-start(f32[8,64,512]{2,1,0:T(8,128)} %broadcast_select_fusion), calls=%async_computation.1 | async-start | bytes 2097152 | tf_op jit(solution)/shard_map/all_to_all | solution.py:531
  10.2 1.4 copy-start.4
  10.2 1.9 copy-start.6
  25.2 1.0 copy-start.2
  26.1 85.5 %all-to-all-start = ((f32[128,3,32,128]{3,2,1,0:T(8,128)}), f32[128,3,32,128]{3,2,1,0:T(8,128)}, u32[]{:S(2)}, u32[]{:S(2)}) async-start(f32[128,3,32,128]{3,2,1,0:T(8,128)} %select_tiles.1), calls=%async_computation | async-start | bytes 12582912 | tf_op jit(solution)/shard_map/all_to_all | solution.py:539
  131.6 8.2 %copy-start.5 = (f32[1024]{0:T(1024)S(1)}, f32[1024]{0:T(1024)}, u32[]{:S(2)}) copy-start(f32[1024]{0:T(1024)} %param.18) | copy-start | bytes 12292
  131.6 48.5 %all-to-all-start.2 = ((f32[128,3,16,128]{3,2,1,0:T(8,128)}), f32[128,3,16,128]{3,2,1,0:T(8,128)S(1)}, u32[]{:S(2)}, u32[]{:S(2)}) async-start(f32[128,3,16,128]{3,2,1,0:T(8,128)} %batch_product.1), calls=%async_computation.2 | async-start | bytes 6291456 | tf_op jit(solution)/shard_map/all_to_all | solution.py:544
  180.2 1.7 copy-start.1

commit v3 on v2

--- a/solution.py
+++ b/solution.py
@@ -34,30 +34,125 @@
     return pl.BlockSpec(memory_space=pltpu.SMEM)
 
 
-def select_kernel(slot_ref, tiles_ref, out_ref):
-    count = out_ref.shape[0]
-
-    def body(n, carry):
-        slot = slot_ref[n]
-        picked = tiles_ref[:, jnp.maximum(slot, 0)]
-        out_ref[n] = jnp.where(slot >= 0, picked, jnp.inf)
+MESH = pl.DeviceIdType.MESH
+
+
+def gather_kernel(
+    slot_ref, asked_ref, tiles_ref, c_ref, out_ref, cout_ref,
+    mate0, mate1, mate2, picked, chosen,
+    mate_send, mate_recv, tile_send, tile_recv, c_send, c_recv,
+):
+    row = lax.axis_index("row")
+    col = lax.axis_index("col")
+    z, y = col // 4, col % 4
+    mates = (mate0, mate1, mate2)
+    mate = (row, z * 4 + (y // 2) * 2 + 1 - y % 2)
+    place = row * 8 + col // 2
+
+    def target(n):
+        t, rest = n % 2, n // 2
+        tz, tr = lax.rem(z + rest % 4, 4), lax.rem(row + rest // 4, 8)
+        return tr, tz * 4 + (1 - t) * y + t * (3 - y)
+
+    barrier = pltpu.get_barrier_semaphore()
+    pl.semaphore_signal(barrier, inc=1, device_id=mate, device_id_type=MESH)
+
+    def greet(n, carry):
+        pl.semaphore_signal(barrier, inc=1, device_id=target(n), device_id_type=MESH)
         return carry
 
-    lax.fori_loop(0, count, body, 0)
-
-
-def select_tiles(slots, tiles):
+    lax.fori_loop(1, 64, greet, 0)
+    for k in range(8):
+        chosen[k] = c_ref[asked_ref[k]]
+    pl.semaphore_wait(barrier, 64)
+
+    exchange = [
+        pltpu.make_async_remote_copy(
+            src_ref=tiles_ref.at[d], dst_ref=mates[d], send_sem=mate_send.at[d],
+            recv_sem=mate_recv.at[d], device_id=mate, device_id_type=MESH,
+        )
+        for d in range(3)
+    ]
+    for copy in exchange:
+        copy.start()
+
+    def orbital_copy(k):
+        to = lax.rem(row + k, 8)
+        return pltpu.make_async_remote_copy(
+            src_ref=chosen.at[to], dst_ref=cout_ref.at[row], send_sem=c_send.at[k],
+            recv_sem=c_recv, device_id=(to, col), device_id_type=MESH,
+        )
+
+    own_orbitals = pltpu.make_async_copy(chosen.at[row], cout_ref.at[row], c_recv)
+    own_orbitals.start()
+    for k in range(1, 8):
+        orbital_copy(k).start()
+
+    def tile_copy(n, d):
+        return pltpu.make_async_remote_copy(
+            src_ref=picked.at[d, n], dst_ref=out_ref.at[place, d], send_sem=tile_send.at[d],
+            recv_sem=tile_recv, device_id=target(n), device_id_type=MESH,
+        )
+
+    for d in range(3):
+        exchange[d].wait_recv()
+
+        def pick(n, carry):
+            slot = slot_ref[n]
+            own = tiles_ref[d, jnp.clip(slot, 0, 31)]
+            other = mates[d][jnp.clip(slot - 32, 0, 31)]
+            value = jnp.where(slot < 32, own, other)
+            picked[d, n] = jnp.where(slot >= 0, value, jnp.inf)
+            return carry
+
+        lax.fori_loop(0, 64, pick, 0)
+        pltpu.make_async_copy(picked.at[d, 0], out_ref.at[place, d], tile_recv).start()
+
+        def send(n, carry):
+            tile_copy(n, d).start()
+            return carry
+
+        lax.fori_loop(1, 64, send, 0)
+
+    pltpu.make_async_copy(out_ref, out_ref, tile_recv).wait()
+    pltpu.make_async_copy(cout_ref, cout_ref, c_recv).wait()
+    for d in range(3):
+        exchange[d].wait_send()
+        rest = picked.at[d, pl.ds(1, 63)]
+        pltpu.make_async_copy(rest, rest, tile_send.at[d]).wait()
+    for k in range(1, 8):
+        orbital_copy(k).wait_send()
+
+
+def gather_tiles(slots, asked, tiles, c_rows):
     return pl.pallas_call(
-        select_kernel,
-        out_shape=jax.ShapeDtypeStruct((slots.shape[0], 3, 32, 128), F32),
-        in_specs=[smem(), vmem()],
-        out_specs=vmem(),
-        name="select_tiles",
-    )(slots, tiles)
+        gather_kernel,
+        out_shape=(
+            jax.ShapeDtypeStruct((64, 3, 32, 128), F32),
+            jax.ShapeDtypeStruct((8, TILE, 512), F32),
+        ),
+        in_specs=[smem(), smem(), vmem(), vmem()],
+        out_specs=(pl.BlockSpec(memory_space=pl.ANY), pl.BlockSpec(memory_space=pl.ANY)),
+        scratch_shapes=[
+            pltpu.VMEM((32, 32, 128), F32),
+            pltpu.VMEM((32, 32, 128), F32),
+            pltpu.VMEM((32, 32, 128), F32),
+            pltpu.VMEM((3, 64, 32, 128), F32),
+            pltpu.VMEM((8, TILE, 512), F32),
+            pltpu.SemaphoreType.DMA((3,)),
+            pltpu.SemaphoreType.DMA((3,)),
+            pltpu.SemaphoreType.DMA((3,)),
+            pltpu.SemaphoreType.DMA,
+            pltpu.SemaphoreType.DMA((8,)),
+            pltpu.SemaphoreType.DMA,
+        ],
+        compiler_params=pltpu.CompilerParams(collective_id=0, has_side_effects=True),
+        name="gather_tiles",
+    )(slots, asked, tiles, c_rows)
 
 
 def batch_kernel(
-    col_ref, t_ref, b_ref, gw_ref, xc_ref, gc_ref, c_ref, out_ref,
+    t_ref, b_ref, gw_ref, xc_ref, gc_ref, c_ref, out_ref,
     bperm, plane, bstack, bside, dcat, acat, hcat, ccat, pot, mask,
 ):
     for i in range(8):
@@ -89,8 +184,8 @@
     def per_direction(d, carry):
         for i in range(8):
             for q in range(4):
-                t0 = t_ref[i * 16 + col_ref[2 * q], d]
-                t1 = t_ref[i * 16 + col_ref[2 * q + 1], d]
+                t0 = t_ref[i * 8 + 2 * q, d]
+                t1 = t_ref[i * 8 + 2 * q + 1, d]
                 listed0 = t0 < jnp.inf
                 listed1 = t1 < jnp.inf
                 t0 = jnp.where(listed0, t0, 0.0)
@@ -143,11 +238,11 @@
     lax.fori_loop(0, 3, per_direction, 0)
 
 
-def batch_product(col, tiles, basis, weight, kernel, coord, c_batch):
+def batch_product(tiles, basis, weight, kernel, coord, c_batch):
     return pl.pallas_call(
         batch_kernel,
         out_shape=jax.ShapeDtypeStruct((128, 3, 16, 128), F32),
-        in_specs=[smem()] + [vmem()] * 6,
+        in_specs=[vmem()] * 6,
         out_specs=vmem(),
         scratch_shapes=[
             pltpu.VMEM((512, 1024), F32),
@@ -162,7 +257,7 @@
             pltpu.VMEM((8, 512), F32),
         ],
         name="batch_product",
-    )(col, tiles, basis, weight, kernel, coord, c_batch)
+    )(tiles, basis, weight, kernel, coord, c_batch)
 
 
 def solve_kernel(place_ref, arrived_ref, diag_ref, energy_ref, out_ref):
@@ -187,9 +282,6 @@
         out_specs=vmem(),
         name="solve",
     )(place, arrived, diag, energy)
-
-
-MESH = pl.DeviceIdType.MESH
 
 
 def spread_kernel(
@@ -522,24 +614,24 @@
 ):
     row = lax.axis_index("row")
     col = lax.axis_index("col")
-    me = row * 16 + col
-    blocks = lax.dynamic_slice_in_dim(batch_blocks, me, 1, 0)[0]
-
+    z, y = col // 4, col % 4
     c_rows = orbitals.reshape(16, TILE, 512)
-    asked = lax.dynamic_index_in_dim(batch_blocks.reshape(8, 16, 8), col, 1, keepdims=False)
-    asked = lax.dynamic_index_in_dim(asked, row, 1, keepdims=False) - row * 16
-    c_batch = lax.all_to_all(
-        jnp.take(c_rows, asked, axis=0), "row", split_axis=0, concat_axis=0, tiled=True
-    )
+
+    pairs = [(c, c // 2 * 2 + 1 - c % 2) for c in range(16)]
+    union = jnp.concatenate([tile_ids, lax.ppermute(tile_ids, "col", pairs)])
     ask_row = lax.dynamic_index_in_dim(batch_blocks, row, 1, keepdims=False)
     ask_col = lax.dynamic_index_in_dim(batch_blocks, col // 2, 1, keepdims=False)
-    match = (ask_row * NBLK + ask_col)[:, None] == tile_ids[None, :]
-    slots = jnp.max(jnp.where(match, jnp.arange(32, dtype=jnp.int32)[None, :], -1), axis=1)
-    outgoing = select_tiles(slots, density_tiles.reshape(3, 32, 32, 128))
-    arrived = lax.all_to_all(outgoing, ("row", "col"), split_axis=0, concat_axis=0, tiled=True)
-
+    match = (ask_row * NBLK + ask_col)[:, None] == union[None, :]
+    slots = jnp.max(jnp.where(match, jnp.arange(64, dtype=jnp.int32)[None, :], -1), axis=1)
+    n = jnp.arange(64, dtype=jnp.int32)
+    served_row = (row + n // 8) % 8
+    served_col = (z + n // 2 % 4) % 4 * 4 + jnp.where(n % 2 == 0, y, 3 - y)
+    slots = jnp.take(slots, served_row * 16 + served_col)
+    asked = lax.dynamic_index_in_dim(ask_row.reshape(8, 16), col, 1, keepdims=False) - row * 16
+
+    arrived, c_batch = gather_tiles(slots, asked, density_tiles.reshape(3, 32, 32, 128), c_rows)
     product = batch_product(
-        blocks // 8, arrived, basis_values, grid_weight, xc_kernel, grid_coord, c_batch
+        arrived, basis_values, grid_weight, xc_kernel, grid_coord, c_batch
     )
     spread = lax.all_to_all(product, ("row", "col"), split_axis=0, concat_axis=0, tiled=True)
     diag = lax.dynamic_index_in_dim(precond_diag.reshape(16, 4, 16), col // 4, 1, keepdims=False)

time: 259 us -> 216 us (0.83)
  waiting for transfers between devices: 121 us -> 39 us
  Pallas kernels: 99.6 us -> 157 us
  starting transfers between devices: 23.5 us -> 8.19 us
    all_to_all x2 -> x0, waiting for transfers between devices: 82 us -> none  [the longest x1 75.2 us: local(): lax.all_to_all(outgoing, ('row', 'col'), split_axis=0, concat_axis=0, til...]
    pallas_call x1, Pallas kernels: 5.69 us -> 63.8 us  [gather_tiles(): pl.pallas_call(gather_kernel, out_shape=(jax.ShapeDtypeStruct((64, 3, 32,...]
    all_to_all x2 -> x0, starting transfers between devices: 15.3 us -> none  [the longest x1 9.51 us: local(): lax.all_to_all(outgoing, ('row', 'col'), split_axis=0, concat_axis=0, til...]
  transfers between devices with their start and end apart: 3 -> 2, of which waited for: 3 -> 1; matrix products, arithmetic and copies ran while one was open for 2% -> 3% of each run, Pallas kernels for 2% -> 0%
where the time goes in v3:
time: 216 us
  Pallas kernels  157 us (73%)
  waiting for transfers between devices  39 us (18%)
  local copies, waits for them, and re-layouts  8.55 us (4%)
  starting transfers between devices  8.19 us (4%)
  other arithmetic  3.43 us (2%)
    pallas_call x1, Pallas kernels, gather_tiles(): pl.pallas_call(gather_kernel, out_shape=(jax.ShapeDtypeStruct((64, 3, 32,...  63.8 us
    pallas_call x1, Pallas kernels, spread_orbitals(): pl.pallas_call(spread_kernel, out_shape=(jax.ShapeDtypeStruct((16, 3, TIL...  45.9 us
    all_to_all x1, waiting for transfers between devices, local(): lax.all_to_all(product, ('row', 'col'), split_axis=0, concat_axis=0, tile...  39 us
    pallas_call x1, Pallas kernels, renew(): pl.pallas_call(renew_kernel, out_shape=jax.ShapeDtypeStruct((3, 32, 32, 1...  24.1 us
    pallas_call x1, Pallas kernels, batch_product(): pl.pallas_call(batch_kernel, out_shape=jax.ShapeDtypeStruct((128, 3, 16,...  19.2 us
    all_to_all x1, starting transfers between devices, local(): lax.all_to_all(product, ('row', 'col'), split_axis=0, concat_axis=0, tile...  6.08 us
  transfers between devices with their start and end apart: 2, of which 1 were waited for; matrix products, arithmetic and copies ran while one was open for 3% of the time, Pallas kernels for 0%

profile of v3, /device:TPU:1, one launch (start us, length us, event | category | flops | bytes accessed | tf_op | source)
XLA Modules:
  0.0 216.1 jit_solution(13522941950871863509)
XLA Ops:
  0.0 0.0 copy-start
  0.0 2.1 collective-permute-start
  2.1 1.3 fusion.23
  3.5 0.1 reshape.236
  3.6 2.8 %copy.11 = f32[12,8,32,128]{3,2,1,0:T(8,128)} copy(f32[12,8,32,128]{3,1,2,0:T(8,128)} %bitcast.20) | data formatting | bytes 3145728
  6.4 0.7 subtract_reduce_fusion.asked_ref
  7.1 0.0 collective-permute-done
  7.1 0.1 pad_add_fusion
  7.2 0.1 select_reduce_fusion
  7.3 0.8 gather_fusion
  8.1 0.6 and_select_fusion.6.slot_ref
  8.7 63.8 %gather_tiles.1 = (f32[64,3,32,128]{3,2,1,0:T(8,128)}, f32[8,64,512]{2,1,0:T(8,128)}) custom-call(s32[64]{0:T(128)} %and_select_fusion.6.slot_ref, s32[8]{0:T(128)} %subtract_reduce_fusion.asked_ref, f32[3,32,32,128]{3,2,1,0:T(8,128)} %bitcast.19, f32[16,64,512]{2,1,0:T(8,128)} %bitcast.16), custom_call_target="tpu_custom_call" | custom-call | tf_op jit(solution)/shard_map/gather_tiles/pallas_call | solution.py:128
  72.5 19.2 %batch_product.1 = f32[128,3,16,128]{3,2,1,0:T(8,128)} custom-call(f32[64,3,32,128]{3,2,1,0:T(8,128)} %get-tuple-element.9.t_ref, f32[1,512,1024]{2,1,0:T(8,128)} %b_ref.1, f32[1,1024]{1,0:T(1,128)} %gw_ref.1, f32[1,1024]{1,0:T(1,128)} %xc_ref.1, f32[3,1,1024]{2,1,0:T(1,128)} %gc_ref.1, f32[8,64,512]{2,1,0:T(8,128)} %get-tuple-element.10.c_ref), custom_call_target="tpu_custom_call" | custom-call | tf_op jit(solution)/shard_map/batch_product/pallas_call | solution.py:242
  91.6 6.1 %all-to-all-start = ((f32[128,3,16,128]{3,2,1,0:T(8,128)}), f32[128,3,16,128]{3,2,1,0:T(8,128)S(1)}, u32[]{:S(2)}, u32[]{:S(2)}) async-start(f32[128,3,16,128]{3,2,1,0:T(8,128)} %batch_product.1), calls=%async_computation | async-start | bytes 6291456 | tf_op jit(solution)/shard_map/all_to_all | solution.py:636
  97.7 0.1 reshape.239
  97.9 0.5 constant_dynamic-slice_fusion.energy_ref
  98.4 0.6 fusion.8
  98.9 39.0 %all-to-all-done.arrived_ref = f32[128,3,16,128]{3,2,1,0:T(8,128)S(1)} async-done(((f32[128,3,16,128]{3,2,1,0:T(8,128)}), f32[128,3,16,128]{3,2,1,0:T(8,128)S(1)}, u32[]{:S(2)}, u32[]{:S(2)}) %all-to-all-start) | async-done | bytes 3145760 | tf_op jit(solution)/shard_map/all_to_all | solution.py:636
  137.9 0.9 broadcast_in_dim.49.diag_ref
  138.8 0.8 copy-done.1
  139.6 3.9 %solve.1.x_ref = f32[16,3,16,128]{3,2,1,0:T(8,128)} custom-call(s32[128]{0:T(128)} %get-tuple-element.15.place_ref, f32[128,3,16,128]{3,2,1,0:T(8,128)} %copy-done.1, f32[16,16,128]{2,1,0:T(8,128)} %broadcast_in_dim.49.diag_ref, f32[1,128]{1,0:T(1,128)} %constant_dynamic-slice_fusion.energy_ref), custom_call_target="tpu_custom_call" | custom-call | tf_op jit(solution)/shard_map/solve/pallas_call | solution.py:278
  143.5 45.9 %spread_orbitals.1 = (f32[16,3,64,512]{3,2,1,0:T(8,128)}, f32[8,4,64,512]{3,2,1,0:T(8,128)}) custom-call(f32[16,3,16,128]{3,2,1,0:T(8,128)} %solve.1.x_ref, f32[16,64,512]{2,1,0:T(8,128)} %bitcast.17), custom_call_target="tpu_custom_call" | custom-call | tf_op jit(solution)/shard_map/spread_orbitals/pallas_call | solution.py:505
  189.4 24.1 %renew.1 = f32[3,32,32,128]{3,2,1,0:T(8,128)} custom-call(s32[32]{0:T(128)} %get-tuple-element.17.row_ref, s32[32]{0:T(128)} %get-tuple-element.16.col_ref, f32[16,3,64,512]{3,2,1,0:T(8,128)} %get-tuple-element.11.xr_ref, f32[8,4,64,512]{3,2,1,0:T(8,128)} %get-tuple-element.12.xc_ref, f32[16,64,512]{2,1,0:T(8,128)} %bitcast.18), custom_call_target="tpu_custom_call" | custom-call | tf_op jit(solution)/shard_map/renew/pallas_call | solution.py:587
  213.5 2.6 %reshape.241 = f32[3,32,4096]{2,1,0:T(8,128)} reshape(f32[3,32,32,128]{3,2,1,0:T(8,128)} %renew.1) | data formatting | bytes 3145728 | tf_op jit(solution)/shard_map/reshape | solution.py:644
  (9 shorter events, 0.1 us)
Async XLA Ops:
  0.0 97.8 %copy-start = (f32[512]{0:T(512)S(1)}, f32[512]{0:T(512)}, u32[]{:S(2)}) copy-start(f32[512]{0:T(512)} %param.19) | copy-start | bytes 6148
  0.0 7.1 %copy-start.3 = (s32[32]{0:T(128)S(1)}, s32[32]{0:T(128)}, u32[]{:S(2)}) copy-start(s32[32]{0:T(128)} %param.11) | copy-start | bytes 388
  0.0 7.1 %collective-permute-start = (s32[32]{0:T(128)}, s32[32]{0:T(128)S(1)}, u32[]{:S(2)}, u32[]{:S(2)}) collective-permute-start(s32[32]{0:T(128)} %param.11), channel_id=1, source_target_pairs={{0,1},{1,0},{2,3},{3,2},{4,5},{5,4},{6,7},{7,6},{8,9},{9,8},{10,11... | collective-permute-start | bytes 392 | tf_op jit(solution)/shard_map/ppermute | solution.py:621
  91.6 6.1 %copy-start.2 = (f32[1024]{0:T(1024)S(1)}, f32[1024]{0:T(1024)}, u32[]{:S(2)}) copy-start(f32[1024]{0:T(1024)} %param.18) | copy-start | bytes 12292
  91.6 46.3 %all-to-all-start = ((f32[128,3,16,128]{3,2,1,0:T(8,128)}), f32[128,3,16,128]{3,2,1,0:T(8,128)S(1)}, u32[]{:S(2)}, u32[]{:S(2)}) async-start(f32[128,3,16,128]{3,2,1,0:T(8,128)} %batch_product.1), calls=%async_computation | async-start | bytes 6291456 | tf_op jit(solution)/shard_map/all_to_all | solution.py:636
  137.9 1.7 copy-start.1
